TPU v7x, 512 devices: a whole 4x4x16 slice. The times are simulated.
512 devices in a mesh: cells: 128 (over z, y, core), mem: 4 (over x).
Axes of the slice: x: 4, y: 4, z: 16, core: 2. Of those that a mesh axis runs over, the one named last changes fastest.
Arguments:
- ensemble: float32 [512, 262144], P('mem', 'cells'), may hold values from -6 to 6
- observed: float32 [262144], P('cells'), may hold values from -6 to 6
- obs_sigma: float32 [262144], P('cells'), may hold values from 0.1 to 1
- obs_index: int32 [262144], P('cells'), may hold values from 0 to 2047
- member_seeds: int32 [512], P('mem'), may hold values from 1 to 65520
Outputs:
- updated: float32 [512, 262144], P('mem', 'cells')
All inputs are finite; a program needn't handle non-finite values.
Results may differ from a plain program's by a relative error of at most 0.0003.
Values sent between devices are 32-bit elements; how exact they have to be, the bound alone decides.
A program may use at most 64 MiB of HBM per device.

v0:
```python
import math

import jax
import jax.numpy as jnp
from jax import lax
from jax.sharding import Mesh
from jax.sharding import PartitionSpec as P

SECTION = 1
CELLS = ("cells_0", "cells_1", "cells_2")


plan = (28.0 / 3.0, 7.0, 4.0, 2.0)


def from_everyone(shard, axis):
    copies = jnp.broadcast_to(shard, (lax.axis_size(axis), *shard.shape))
    return lax.all_to_all(copies, axis, split_axis=0, concat_axis=0, tiled=True)


def over_copies(shard, axis):
    return from_everyone(shard, axis).sum(axis=0)


def together(arrays, axis):
    ends = [0]
    for a in arrays:
        ends.append(ends[-1] + a.size)
    total = over_copies(jnp.concatenate([a.ravel() for a in arrays]), axis)
    return tuple((total[b:e].reshape(a.shape) for a, b, e in zip(arrays, ends, ends[1:])))


def rows_for(lines, devices):
    spare = -len(lines) % devices
    return jnp.pad(lines, [(0, spare)] + [(0, 0)] * (lines.ndim - 1))


def laid_out(tiles, dim):
    tiles = jnp.moveaxis(tiles, 0, dim)
    lengths = tiles.shape
    return tiles.reshape(*lengths[:dim], lengths[dim] * lengths[dim + 1], *lengths[dim + 2 :])


def gather_axes(shard, axes, dim):
    far, near = axes
    leading = from_everyone(shard, far)
    tiles = jnp.swapaxes(from_everyone(leading, near), 0, 1)
    return laid_out(tiles.reshape(-1, *shard.shape), dim)


def in_blocks(shard, dim, devices):
    lengths = shard.shape
    tiles = shard.reshape(*lengths[:dim], devices, lengths[dim] // devices, *lengths[dim + 1 :])
    return jnp.moveaxis(tiles, dim, 0)


def summed_on_arrival(shard, axis, dim):
    devices = lax.axis_size(axis)
    tiles = lax.all_to_all(in_blocks(shard, dim, devices), axis, 0, 0, tiled=True)
    return jnp.sum(tiles, axis=0)


def summed_rows(shard, axes, dim):
    far, near = axes
    tiles = in_blocks(shard, dim, lax.axis_size(far))
    nearer = summed_on_arrival(tiles, near, dim + 1)
    arrived = lax.all_to_all(nearer, far, split_axis=0, concat_axis=0, tiled=True)
    return arrived.sum(axis=0)


def nested_sum(shard, axes):
    padded = rows_for(shard, lax.axis_size(axes[0]) * lax.axis_size(axes[1]))
    whole = gather_axes(summed_rows(padded, axes, 0), axes, 0)
    return lax.slice_in_dim(whole, 0, len(shard)).reshape(shard.shape)


def together_2(arrays, axis):
    ends = [0]
    for a in arrays:
        ends.append(ends[-1] + a.size)
    total = nested_sum(jnp.concatenate([a.ravel() for a in arrays]), axis)
    return tuple((total[b:e].reshape(a.shape) for a, b, e in zip(arrays, ends, ends[1:])))


def perturbation(member_seeds, positions):
    seeds_col = member_seeds[:, None]
    where_row = positions[None, :]
    hashed = (seeds_col * 389 % 65521 + where_row % 65521 * (seeds_col % 997 + 1)) % 65521
    return math.sqrt(2.0) * jnp.cos(2.0 * math.pi / 65521.0 * hashed.astype(jnp.float32))


def shards(ensemble, observed, obs_sigma, obs_index, member_seeds):
    highest = lax.Precision.HIGHEST
    own_members, cell_count = ensemble.shape
    obs_count = observed.shape[0]
    members = own_members * lax.axis_size("mem")
    alpha = jnp.float32(plan[SECTION])
    value = ensemble[:, obs_index]
    predicted = jnp.tanh(value) + 0.5 * value
    totals = together((jnp.sum(ensemble, axis=0), jnp.sum(predicted, axis=0)), "mem")
    mean_state = totals[0] / members
    mean_pred = totals[1] / members
    positions = lax.axis_index(CELLS) * obs_count + jnp.arange(obs_count, dtype=jnp.int32)
    noise = perturbation(member_seeds, positions)
    scaled = (predicted - mean_pred) / (obs_sigma * math.sqrt(members - 1.0))
    innovation = observed / obs_sigma + jnp.sqrt(alpha) * noise - predicted / obs_sigma
    gathered = lax.all_gather(scaled, "mem", axis=0, tiled=True)
    gram_matrix, cross_terms = together_2(
        (
            jnp.dot(gathered, gathered.T, precision=highest),
            jnp.dot(gathered, innovation.T, precision=highest),
        ),
        (("cells_0", "cells_1"), "cells_2"),
    )
    factor = jnp.linalg.cholesky(gram_matrix + alpha * jnp.eye(members, dtype=jnp.float32))
    weights = jax.scipy.linalg.cho_solve((factor, True), cross_terms)
    anomalies = ensemble - mean_state
    change = jnp.zeros((own_members, cell_count), jnp.float32) + jnp.dot(
        weights.T, lax.all_gather(anomalies, "mem", axis=0, tiled=True), precision=highest
    )
    return ensemble + change / math.sqrt(members - 1.0)


def solution(mesh):
    finer = Mesh(
        mesh.devices.reshape(16, 4, 2, mesh.shape["mem"]), ("cells_0", "cells_1", "cells_2", "mem")
    )
    placed = (P("mem", CELLS), P(CELLS), P(CELLS), P(CELLS), P("mem"))
    return jax.shard_map(
        shards, mesh=finer, in_specs=placed, out_specs=P("mem", CELLS), check_vma=False
    )
```

profile of v0, /device:TPU:1, one launch (start us, length us, event | category | flops | bytes accessed | tf_op | source)
XLA Modules:
  0.0 412.3 jit_solution(3694493013845789510)
XLA Ops:
  6.5 1.6 copy.68
  8.1 5.5 %gather_fusion = f32[2048,128]{1,0:T(8,128)S(1)} fusion(f32[128,2048]{0,1:T(8,128)S(1)} %copy.68, s32[2048]{0:T(1024)S(1)} %fusion.75), kind=kCustom, calls=%fused_computation | custom fusion | bytes 2105344 | tf_op jit(solution)/shard_map/gather | solution.py:98
  15.0 9.1 %all_to_all.34 = f32[4,1,4096]{2,1,0:T(1,128)S(1)} all-to-all(f32[4,1,4096]{2,1,0:T(1,128)S(1)} %broadcast_in_dim.10), channel_id=1, replica_groups=mesh['cells_0'=16,'cells_1'=4,'cells_2'=2,'mem'=4] {'mem'}, dimensions={0} | all-to-all | bytes 131072 | tf_op jit(solution)/shard_map/all_to_all | solution.py:18
  24.2 1.5 divide_bitcast_fusion
  25.8 61.8 %all-gather.3.cloned.1.call-done = f32[512,2048]{0,1:T(8,128)} async-done(((f32[128,2048]{0,1:T(8,128)}), f32[512,2048]{0,1:T(8,128)}) %all-gather.3.cloned.1.call-update) | async-done | bytes 4194320 | tf_op jit(solution)/shard_map/all_gather | solution.py:107
  87.6 10.6 %convolution_bitcast_fusion.1 = f32[64,4,8,128]{3,2,1,0:T(8,128)S(1)} fusion(f32[512,2048]{0,1:T(8,128)} %all-gather.3.cloned.1.call-done), kind=kOutput, calls=%fused_computation.7 | convolution fusion | flops 6442450944 | bytes 5242880 | tf_op jit(solution)/shard_map/dot_general | solution.py:110
  98.4 10.8 %convolution_bitcast_fusion = f32[65536]{0:T(1024)S(1)} fusion(f32[512,2048]{0,1:T(8,128)S(1)} %copy-done, f32[2048,128]{1,0:T(8,128)S(1)} %gather_fusion, f32[2048]{0:T(1024)S(1)} %copy-done.6, s32[128]{0:T(128)S(1)} %get-tuple-element.58, s32[2048]{0:T(1024)S(1)} %add_select_fusion.1, s32[128]{0:T(128)S(1)} %get-tuple-element.57, ...), kind=kOutput, calls=%fused_computation.3 | convolution fusion | flops 1614807040 | bytes 5530624 | tf_op jit(solution)/shard_map/dot_general | solution.py:111
  109.3 1.8 reshape_reshape.4
  111.0 1.6 copy.70
  112.6 6.9 %all_to_all.35 = f32[2,64,2560]{2,1,0:T(8,128)S(1)} all-to-all(f32[2,64,2560]{2,1,0:T(8,128)S(1)} %copy.70), channel_id=1, replica_groups=mesh['cells_0'=16,'cells_1'=4,'cells_2'=2,'mem'=4] {'cells_2'}, dimensions={0} | all-to-all | bytes 2621440 | tf_op jit(solution)/shard_map/all_to_all | solution.py:59
  120.1 51.2 %all_to_all.36 = f32[64,1,2560]{2,1,0:T(1,128)S(1)} all-to-all(f32[64,1,2560]{2,1,0:T(1,128)S(1)} %all_to_all.24), channel_id=1, replica_groups=mesh['cells_0'=16,'cells_1'=4,'cells_2'=2,'mem'=4] {'cells_0','cells_1'}, dimensions={0} | all-to-all | bytes 1310720 | tf_op jit(solution)/shard_map/all_to_all | solution.py:67
  171.6 1.2 broadcast_in_dim.12
  172.8 7.9 %all-to-all-start.3 = ((f32[64,1,2560]{2,1,0:T(1,128)}), f32[64,1,2560]{2,1,0:T(1,128)S(1)}, u32[]{:S(2)}, u32[]{:S(2)}) async-start(f32[64,1,2560]{2,1,0:T(1,128)} %broadcast_in_dim.12), calls=%async_computation.3 | async-start | bytes 1310720 | tf_op jit(solution)/shard_map/all_to_all | solution.py:18
  181.9 33.7 %all-to-all-done.3 = f32[64,1,2560]{2,1,0:T(1,128)S(1)} async-done(((f32[64,1,2560]{2,1,0:T(1,128)}), f32[64,1,2560]{2,1,0:T(1,128)S(1)}, u32[]{:S(2)}, u32[]{:S(2)}) %all-to-all-start.3) | async-done | bytes 655392 | tf_op jit(solution)/shard_map/all_to_all | solution.py:18
  215.7 8.9 %all_to_all.37 = f32[2,64,2560]{2,1,0:T(8,128)S(1)} all-to-all(f32[2,64,2560]{2,1,0:T(8,128)S(1)} %broadcast_in_dim.24), channel_id=1, replica_groups=mesh['cells_0'=16,'cells_1'=4,'cells_2'=2,'mem'=4] {'cells_2'}, dimensions={0} | all-to-all | bytes 2621440 | tf_op jit(solution)/shard_map/all_to_all | solution.py:18
  225.7 2.1 slice.179
  227.8 2.3 slice.197
  230.1 1.6 copy.89
  231.7 1.1 select_add_fusion
  232.8 2.6 copy.73
  235.3 1.4 fusion.8
  237.8 11.7 %cholesky.103 = f32[128,128]{1,0:T(8,128)S(1)} custom-call(f32[128,128]{1,0:T(8,128)S(1)} %cholesky.263), custom_call_target="Cholesky" | custom-call | tf_op jit(solution)/shard_map/jit(cholesky)/cholesky | solution.py:115
  249.6 9.8 %custom-call.34 = f32[1,128,128]{1,2,0:T(8,128)S(1)} custom-call(f32[1,128,128]{2,1,0:T(8,128)S(1)} %get-tuple-element.52), custom_call_target="InvertDiagBlocksLowerTriangular" | custom-call | tf_op jit(solution)/shard_map/jit(cholesky)/cholesky | solution.py:115
  259.4 1.2 fusion.37
  260.6 1.3 convolution_subtract_fusion
  262.6 11.8 %cholesky.215 = f32[128,128]{1,0:T(8,128)S(1)} custom-call(f32[128,128]{1,0:T(8,128)S(1)} %cholesky.267), custom_call_target="Cholesky" | custom-call | tf_op jit(solution)/shard_map/jit(cholesky)/cholesky | solution.py:115
  276.2 10.6 %custom-call.35 = f32[1,128,128]{1,2,0:T(8,128)S(1)} custom-call(f32[1,128,128]{2,1,0:T(8,128)} %get-tuple-element.50), custom_call_target="InvertDiagBlocksLowerTriangular" | custom-call | tf_op jit(solution)/shard_map/jit(cholesky)/cholesky | solution.py:115
  287.8 1.2 convolution_dynamic-update-slice_fusion
  289.0 1.5 convolution_subtract_fusion.1
  291.2 13.2 %cholesky.236 = f32[128,128]{1,0:T(8,128)} custom-call(f32[128,128]{1,0:T(8,128)} %cholesky.272), custom_call_target="Cholesky" | custom-call | tf_op jit(solution)/shard_map/jit(cholesky)/cholesky | solution.py:115
  304.3 1.5 select_reduce_fusion.1
  305.8 1.6 copy.78
  308.2 11.3 %custom-call.36 = f32[1,128,128]{1,2,0:T(8,128)} custom-call(f32[1,128,128]{2,1,0:T(8,128)} %get-tuple-element.48), custom_call_target="InvertDiagBlocksLowerTriangular" | custom-call | tf_op jit(solution)/shard_map/jit(cholesky)/cholesky | solution.py:115
  319.5 1.1 convolution_dynamic-update-slice_fusion.1
  320.6 2.1 slice.181
  322.7 1.5 convolution_subtract_fusion.8
  324.3 11.7 %cholesky.253 = f32[128,128]{1,0:T(8,128)S(1)} custom-call(f32[128,128]{1,0:T(8,128)S(1)} %convolution_subtract_fusion.8), custom_call_target="Cholesky" | custom-call | tf_op jit(solution)/shard_map/jit(cholesky)/cholesky | solution.py:115
  341.1 10.8 %while.1 = (s32[]{:T(128)}, f32[512,512]{0,1:T(8,128)S(1)}, s32[4,2]{0,1:T(2,128)S(1)}, f32[4,128,128]{2,1,0:T(8,128)}, s32[]{:T(128)}) while((s32[]{:T(128)}, f32[512,512]{0,1:T(8,128)S(1)}, s32[4,2]{0,1:T(2,128)S(1)}, f32[4,128,128]{2,1,0:T(8,128)}, s32[]{:T(128)}) %tuple.33), condition=%wide.while_cond, body=%wide.while_body.sunk | while | flops 2 | bytes 393829 | solution.py:116
  341.8 1.3 dynamic-slice.7
  344.5 1.3 dynamic-slice.7
  347.2 1.3 dynamic-slice.7
  349.9 1.3 dynamic-slice.7
  351.9 40.4 %custom-call.37 = f32[4,128,128]{1,2,0:T(8,128)S(1)} custom-call(f32[4,128,128]{2,1,0:T(8,128)} %get-tuple-element.12), custom_call_target="InvertDiagBlocksLowerTriangular" | custom-call | tf_op jit(solution)/shard_map/jit(_cho_solve)/triangular_solve | solution.py:116
  392.3 1.1 fusion.61
  393.4 1.1 convolution_subtract_fusion.5
  394.8 1.2 convolution_subtract_fusion.4
  396.4 1.3 convolution_subtract_fusion.7
  399.7 5.5 %fusion = f32[128,2048]{1,0:T(8,128)} fusion(f32[128,2048]{1,0:T(8,128)S(1)} %copy-done.1, f32[512,2048]{1,0:T(8,128)} %all-gather.5.cloned.1.call-done, f32[128,128]{1,0:T(8,128)S(1)} %fusion.73, f32[128,128]{1,0:T(8,128)S(1)} %fusion.71, f32[128,128]{1,0:T(8,128)S(1)} %fusion.69, f32[128,128]{1,0:T(8,128)S(1)} %fusion.68), kind=kOutput, calls=%fused_computation.5 | convolution fusion | flops 1611333632 | bytes 6553600 | tf_op jit(solution)/shard_map/dot_general | solution.py:118
  (88 shorter events, 21.7 us)
Async XLA Ops:
  6.5 1.6 copy-start.4
  6.5 81.0 %all-gather.3.cloned.1.call-start = ((), (), s32[]{:S(2)}) async-start(), calls=%async_computation.5 | async-start | bytes 5242880 | tf_op jit(solution)/shard_map/all_gather | solution.py:107
  13.6 1.2 copy-start.1
  13.6 10.5 %copy-start.5 = (f32[2048]{0:T(1024)S(1)}, f32[2048]{0:T(1024)}, u32[]{:S(2)}) copy-start(f32[2048]{0:T(1024)} %param.6) | copy-start | bytes 24580
  13.6 10.5 %copy-start.6 = (f32[2048]{0:T(1024)S(1)}, f32[2048]{0:T(1024)}, u32[]{:S(2)}) copy-start(f32[2048]{0:T(1024)} %param.7) | copy-start | bytes 24580
  24.2 1.6 copy-start.7
  87.6 10.9 %copy-start = (f32[512,2048]{0,1:T(8,128)S(1)}, f32[512,2048]{0,1:T(8,128)}, u32[]{:S(2)}) copy-start(f32[512,2048]{0,1:T(8,128)} %all-gather.3.cloned.1.call-done) | copy-start | bytes 12582916
  172.8 42.8 %all-to-all-start.3 = ((f32[64,1,2560]{2,1,0:T(1,128)}), f32[64,1,2560]{2,1,0:T(1,128)S(1)}, u32[]{:S(2)}, u32[]{:S(2)}) async-start(f32[64,1,2560]{2,1,0:T(1,128)} %broadcast_in_dim.12), calls=%async_computation.3 | async-start | bytes 1310720 | tf_op jit(solution)/shard_map/all_to_all | solution.py:18
  180.7 219.0 %all-gather.5.cloned.1.call-start = ((), (), s32[]{:S(2)}) async-start(), calls=%async_computation.6 | async-start | bytes 5242880 | tf_op jit(solution)/shard_map/all_gather | solution.py:119
  236.8 1.0 copy-start.2
  261.9 0.7 copy-start.3
Sparse Core Ops, SparseCore 0:
  25.8 61.6 all-gather.2
  183.6 56.8 all-gather.4
where the time goes:
time: 418 us; the launch traced here: 412 us
  other arithmetic  132 us (32%)
  waiting for transfers between devices  95.6 us (23%)
  blocking collectives  76 us (18%)
  local copies, waits for them, and re-layouts  42.6 us (10%)
  matrix products  41.9 us (10%)
  between operations  16.5 us (4%)
  starting transfers between devices  7.93 us (2%)
    another operation x15, other arithmetic, shards(): jnp.linalg.cholesky(gram_matrix + alpha * jnp.eye(members, dtype=jnp.floa...  84.9 us
    all_gather x1, waiting for transfers between devices, shards(): gathered = lax.all_gather(scaled, 'mem', axis=0, tiled=True)  61.8 us
    all_to_all x1, blocking collectives, summed_rows(): lax.all_to_all(nearer, far, split_axis=0, concat_axis=0, tiled=True)  51.2 us
    another operation x3, other arithmetic, shards(): weights = jax.scipy.linalg.cho_solve((factor, True), cross_terms)  40.5 us
    all_to_all x1, waiting for transfers between devices, from_everyone(): return lax.all_to_all(copies, axis, split_axis=0, concat_axis=0, tiled=True)  33.7 us
    all_to_all x2, blocking collectives, from_everyone(): return lax.all_to_all(copies, axis, split_axis=0, concat_axis=0, tiled=True)  18 us
    dot_general x1, matrix products, shards(): jnp.dot(gathered, innovation.T, precision=highest)  10.8 us
    another operation x20, local copies, waits for them, and re-layouts  10.7 us
  transfers between devices with their start and end apart: 3, of which 2 were waited for; matrix products, arithmetic and copies ran while one was open for 42% of the time, Pallas kernels for 0%

commit v1 on v0

v1 whole, which is shorter than its diff:
```python
import functools
import math

import jax
import jax.numpy as jnp
from jax import lax
from jax.experimental import pallas as pl
from jax.experimental.pallas import tpu as pltpu
from jax.sharding import Mesh
from jax.sharding import PartitionSpec as P

SECTION = 1
CELLS = ("cells_0", "cells_1", "cells_2")
AXES = ("cells_0", "cells_1", "cells_2", "mem")
PLAN = (28.0 / 3.0, 7.0, 4.0, 2.0)
HI = lax.Precision.HIGHEST
MESH = pl.DeviceIdType.MESH
VM = pl.BlockSpec(memory_space=pltpu.VMEM)
ANY = pl.BlockSpec(memory_space=pl.ANY)
F32 = jnp.float32


def remote(src, dst, send, recv, where):
    return pltpu.make_async_remote_copy(
        src_ref=src, dst_ref=dst, send_sem=send, recv_sem=recv, device_id=where, device_id_type=MESH
    )


def at_axis(axis, index):
    return {axis: index}


def greet(peers):
    barrier = pltpu.get_barrier_semaphore()
    for peer in peers:
        pl.semaphore_signal(barrier, inc=1, device_id=peer, device_id_type=MESH)
    pl.semaphore_wait(barrier, len(peers))


def order_of(n):
    return sorted(range(1, n), key=lambda d: -min(d, n - d))


def exchange_kernel(nx, p_ref, s_ref, o_ref, so_ref, send, recv, own):
    x = lax.axis_index("mem")
    rows, width = p_ref.shape[0], p_ref.shape[1] // nx
    greet([at_axis("mem", lax.rem(x + d, nx)) for d in range(1, nx)])
    mine = pl.ds(pl.multiple_of(x * rows, rows), rows)
    copies = []
    for d in order_of(nx):
        to = lax.rem(x + d, nx)
        copies.append(remote(s_ref, so_ref.at[x], send.at[1, d], recv.at[1, d], at_axis("mem", to)))
        cols = pl.ds(pl.multiple_of(to * width, width), width)
        copies.append(remote(p_ref.at[:, cols], o_ref.at[mine, :], send.at[0, d], recv.at[0, d], at_axis("mem", to)))
    for c in copies:
        c.start()
    a = pltpu.make_async_copy(p_ref.at[:, pl.ds(pl.multiple_of(x * width, width), width)], o_ref.at[mine, :], own.at[0])
    b = pltpu.make_async_copy(s_ref, so_ref.at[x], own.at[1])
    a.start()
    b.start()
    a.wait()
    b.wait()
    for c in copies:
        c.wait()


def exchange(predicted, seeds, nx):
    rows, width = predicted.shape
    return pl.pallas_call(
        functools.partial(exchange_kernel, nx),
        out_shape=(
            jax.ShapeDtypeStruct((rows * nx, width // nx), F32),
            jax.ShapeDtypeStruct((nx, 8, rows), F32),
        ),
        in_specs=[VM, VM],
        out_specs=(VM, VM),
        scratch_shapes=[pltpu.SemaphoreType.DMA((2, nx))] * 2 + [pltpu.SemaphoreType.DMA((2,))],
        compiler_params=pltpu.CompilerParams(collective_id=0, has_side_effects=True),
        name="exchange",
    )(predicted, seeds)


def mod_prime(v):
    q = jnp.floor(v.astype(F32) * (1.0 / 65521.0)).astype(jnp.int32)
    r = v - q * 65521
    r = jnp.where(r < 0, r + 65521, r)
    return jnp.where(r >= 65521, r - 65521, r)


def cosine(h):
    h = jnp.minimum(h, 65521 - h)
    v = (65521 - 4 * h).astype(F32) * (math.pi / (2.0 * 65521.0))
    s = v * v
    poly = jnp.full_like(s, -1.0 / 39916800.0)
    for k in (9, 7, 5, 3, 1):
        poly = poly * s + (-1.0) ** ((k - 1) // 2) / math.factorial(k)
    return poly * v


def local_kernel(nx, alpha, p_ref, s_ref, ob_ref, sg_ref, gp_ref, dp_ref, sc, mm):
    members, width = p_ref.shape
    mean = jnp.sum(p_ref[...], axis=0, keepdims=True) * (1.0 / members)
    x = lax.axis_index("mem")
    part = pl.ds(pl.multiple_of(x * width, width), width)
    inv = 1.0 / sg_ref[:, part]
    scale = inv * (1.0 / math.sqrt(members - 1.0))
    shift = (ob_ref[:, part] - mean) * inv
    base = lax.axis_index(CELLS) * ob_ref.shape[1] + x * width
    where = mod_prime(lax.broadcasted_iota(jnp.int32, (1, width), 1) + base)
    reps = p_ref.shape[1] // 128

    def block(b, _):
        rows = pl.ds(pl.multiple_of(b * 128, 128), 128)
        seed = jnp.broadcast_to(s_ref[b, 0:1, :], (128, 128)).T.astype(jnp.int32)
        first = mod_prime(seed * 389)
        second = seed - 997 * jnp.floor((seed.astype(F32) + 0.5) * (1.0 / 997.0)).astype(jnp.int32) + 1
        sc[rows, :] = (p_ref[rows, :] - mean) * scale
        for c in range(reps):
            cols = slice(128 * c, 128 * c + 128)
            h = mod_prime(first + where[:, cols] * second)
            mm[rows, cols] = cosine(h) * math.sqrt(2.0 * alpha) + shift[:, cols]
        return 0

    lax.fori_loop(0, members // 128, block, 0)
    dn = (((1,), (1,)), ((), ()))

    def product(b, _):
        rows = pl.ds(pl.multiple_of(b * 128, 128), 128)
        left = sc[rows, :]
        groups = pl.ds(pl.multiple_of(b * 16, 16), 16)
        half, within = b // 2, pl.ds(pl.multiple_of(lax.rem(b, 2) * 16, 16), 16)
        for c in range(members // 128):
            cols = pl.ds(128 * c, 128)
            g = lax.dot_general(left, sc[cols, :], dn, precision=HI, preferred_element_type=F32)
            gp_ref[groups, c] = g.reshape(16, 8, 128)
            d = lax.dot_general(left, mm[cols, :], dn, precision=HI, preferred_element_type=F32)
            dp_ref[half, c, within] = d.reshape(16, 8, 128)
        return 0

    lax.fori_loop(0, members // 128, product, 0)


def local_products(pred, seeds, obs, sigma, nx, alpha):
    members, width = pred.shape
    return pl.pallas_call(
        functools.partial(local_kernel, nx, alpha),
        out_shape=(
            jax.ShapeDtypeStruct((members // 8, members // 128, 8, 128), F32),
            jax.ShapeDtypeStruct((2, members // 128, members // 16, 8, 128), F32),
        ),
        in_specs=[VM] * 4,
        out_specs=(VM, VM),
        scratch_shapes=[pltpu.VMEM((members, width), F32)] * 2,
        name="local_products",
    )(pred, seeds, obs, sigma)


def reduce_kernel(n, gp, dp, e_ref, go, do, left, right, rg0, rd0, sg0, sd0, rg1, rd1, sg1, sd1, rg2, rd2, zs, rz, zg,
                  cs, cr, xs, xr, ys, yr, zss, zsr, es, er):
    nx, ny, nz = n
    z, y, c, x = (lax.axis_index(a) for a in AXES)
    oc = 1 - c

    def xat(d):
        return lax.rem(x + d, nx)

    def yat(d):
        return lax.rem(y + d, ny)

    def zat(d):
        return lax.rem(z + d, nz)

    core = at_axis("cells_2", oc)
    greet(
        [core]
        + [at_axis("mem", xat(d)) for d in range(1, nx)]
        + [at_axis("cells_1", yat(d)) for d in range(1, ny)]
        + [at_axis("cells_0", zat(d)) for d in range(1, nz)]
    )
    ox, oy, oz = order_of(nx) + [0], order_of(ny) + [0], order_of(nz)
    sent = []

    def go_(copy):
        copy.start()
        sent.append(copy)
        return copy

    c0d, c0g = {}, {}
    for i in range(max(nx, ny)):
        if i < nx:
            d = ox[i]
            c0d[d] = go_(remote(dp.at[oc, xat(d)], rd0.at[xat(d)], cs.at[0, d], cr.at[0, d], core))
        if i < ny:
            d = oy[i]
            c0g[d] = go_(remote(gp.at[oc, yat(d)], rg0.at[yat(d)], cs.at[1, d], cr.at[1, d], core))
    d1, g1 = {}, {}
    for i in range(max(nx, ny)):
        if i < nx:
            d = ox[i]
            c0d[d].wait_recv()
            sd0[xat(d)] = dp[c, xat(d)] + rd0[xat(d)]
            if d:
                d1[d] = go_(remote(sd0.at[xat(d)], rd1.at[d], xs.at[0, d], xr.at[0, d], at_axis("mem", xat(d))))
        if i < ny:
            d = oy[i]
            c0g[d].wait_recv()
            sg0[yat(d)] = gp[c, yat(d)] + rg0[yat(d)]
            if d:
                g1[d] = go_(remote(sg0.at[yat(d)], rg1.at[d], ys.at[0, d], yr.at[0, d], at_axis("cells_1", yat(d))))
    d2, g2 = {}, {}
    for d in ox[:-1]:
        d1[d].wait_recv()
    for d in oy:
        total = sd0[x, yat(d)]
        for k in range(1, nx):
            total = total + rd1[k, yat(d)]
        sd1[yat(d)] = total
        if d:
            d2[d] = go_(remote(sd1.at[yat(d)], rd2.at[d], ys.at[1, d], yr.at[1, d], at_axis("cells_1", yat(d))))
    for d in oy[:-1]:
        g1[d].wait_recv()
    for d in ox:
        total = sg0[y, xat(d)]
        for k in range(1, ny):
            total = total + rg1[k, xat(d)]
        sg1[xat(d)] = total
        if d:
            g2[d] = go_(remote(sg1.at[xat(d)], rg2.at[d], xs.at[1, d], xr.at[1, d], at_axis("mem", xat(d))))
    half = e_ref.shape[0] // 2
    eo = []
    for h in range(2):
        part = e_ref.at[pl.ds(h * half, half), :]
        eo.append(go_(remote(part, left.at[h], es.at[0, h], er.at[0, h], at_axis("mem", xat(1)))))
        eo.append(go_(remote(part, right.at[h], es.at[1, h], er.at[1, h], at_axis("mem", xat(nx - 1)))))
    for d in oy[:-1]:
        d2[d].wait_recv()
    td, tg = sd1.shape[1], sg1.shape[1]
    q = zs.shape[1]
    total = sd1[y]
    for k in range(1, ny):
        total = total + rd2[k]
    for t in range(td):
        zs[t // q, t % q] = total[t]
    for d in ox[:-1]:
        g2[d].wait_recv()
    total = sg1[x]
    for k in range(1, nx):
        total = total + rg2[k]
    for t in range(tg):
        zs[(td + t) // q, (td + t) % q] = total[t]
    z1 = [go_(remote(zs.at[zat(d)], rz.at[d], zss.at[0, d], zsr.at[0, d], at_axis("cells_0", zat(d)))) for d in oz]
    for w in z1:
        w.wait_recv()
    total = zs[z]
    for k in range(1, nz):
        total = total + rz[k]
    zg[z] = total
    z2 = [go_(remote(zg.at[z], zg.at[z], zss.at[1, d], zsr.at[1, d], at_axis("cells_0", zat(d)))) for d in oz]
    for w in z2:
        w.wait_recv()
    nd = td // q
    for t in range(td):
        do[c, y, t // q, t % q] = zg[t // q, t % q]
    for t in range(tg):
        go[c, y, x, t // q, t % q] = zg[nd + t // q, t % q]
    dy, gx, gy = {}, {}, {}
    for d in ox[:-1]:
        gx[d] = go_(remote(zg.at[pl.ds(nd, tg // q)], go.at[c, y, x], xs.at[2, d], xr.at[2, d], at_axis("mem", xat(d))))
    for d in oy[:-1]:
        dy[d] = go_(remote(zg.at[pl.ds(0, nd)], do.at[c, y], ys.at[2, d], yr.at[2, d], at_axis("cells_1", yat(d))))
    last = [go_(remote(zg.at[pl.ds(0, nd)], do.at[c, y], cs.at[2, 0], cr.at[2, 0], core))]
    for d in ox[:-1]:
        gx[d].wait_recv()
    for d in oy[:-1]:
        gy[d] = go_(remote(go.at[c, y], go.at[c, y], ys.at[3, d], yr.at[3, d], at_axis("cells_1", yat(d))))
    last.append(go_(remote(go.at[c, y], go.at[c, y], cs.at[3, 0], cr.at[3, 0], core)))
    for d in sorted(oy[:-1]):
        frm = yat(ny - d)
        dy[d].wait_recv()
        last.append(go_(remote(do.at[c, frm], do.at[c, frm], cs.at[2, d], cr.at[2, d], core)))
    for d in (1, ny - 1) + tuple(range(2, ny - 1)):
        if d in gy:
            frm = yat(ny - d)
            g = gy.pop(d)
            g.wait_recv()
            last.append(go_(remote(go.at[c, frm], go.at[c, frm], cs.at[3, d], cr.at[3, d], core)))
    for w in last:
        w.wait_recv()
    for w in eo:
        w.wait_recv()
    for w in sent:
        w.wait_send()


def reduce_all(gp, dp, e, nx, ny, nz):
    tg, td = gp.shape[3], dp.shape[3]
    q = (tg + td) // nz
    tile = (8, 128)
    m = max(nx, ny)
    half = (2, e.shape[0] // 2, e.shape[1])
    dma = pltpu.SemaphoreType.DMA
    return pl.pallas_call(
        functools.partial(reduce_kernel, (nx, ny, nz)),
        out_shape=(
            jax.ShapeDtypeStruct((2, ny, nx, tg // q, q, *tile), F32),
            jax.ShapeDtypeStruct((2, ny, td // q, q, *tile), F32),
            jax.ShapeDtypeStruct(half, F32),
            jax.ShapeDtypeStruct(half, F32),
        ),
        in_specs=[VM, VM, ANY],
        out_specs=(VM, VM, ANY, ANY),
        scratch_shapes=[
            pltpu.VMEM((ny, nx, tg, *tile), F32),
            pltpu.VMEM((nx, ny, td, *tile), F32),
            pltpu.VMEM((ny, nx, tg, *tile), F32),
            pltpu.VMEM((nx, ny, td, *tile), F32),
            pltpu.VMEM((ny, nx, tg, *tile), F32),
            pltpu.VMEM((nx, ny, td, *tile), F32),
            pltpu.VMEM((nx, tg, *tile), F32),
            pltpu.VMEM((ny, td, *tile), F32),
            pltpu.VMEM((nx, tg, *tile), F32),
            pltpu.VMEM((ny, td, *tile), F32),
            pltpu.VMEM((nz, q, *tile), F32),
            pltpu.VMEM((nz, q, *tile), F32),
            pltpu.VMEM((nz, q, *tile), F32),
            dma((4, m)), dma((4, m)), dma((3, nx)), dma((3, nx)), dma((4, ny)), dma((4, ny)), dma((2, nz)), dma((2, nz)),
            dma((2, 2)), dma((2, 2)),
        ],
        compiler_params=pltpu.CompilerParams(collective_id=1, has_side_effects=True),
        name="reduce_all",
    )(gp, dp, e)


def factor_block(blk):
    lane = lax.broadcasted_iota(jnp.int32, (8, 128), 1)
    sub = lax.broadcasted_iota(jnp.int32, (8, 128), 0)
    n = list(blk)
    dv = [None] * 16
    def lb(x, c):
        return jnp.broadcast_to(x[:, c:c + 1], (8, 128))
    def sb(x, k):
        return jnp.broadcast_to(x[k:k + 1, :], (8, 128))
    for p in range(16):
        base = 8 * p
        t = [lb(n[p], base + k) for k in range(8)]
        mult = {}
        rows = []
        cur = n[p]
        dvp = None
        for k in range(8):
            rec = 1.0 / sb(t[k], k)
            low = jnp.where(sub > k, t[k], 0.0)
            at = lane == base + k
            r = sb(cur, k)
            sr = jnp.where(at, rec, r * rec)
            rows.append(sr if k == 7 else jnp.where((lane > base + k) & (lane < base + 8), 0.0, sr))
            dvp = rec if dvp is None else jnp.where(sub == k, rec, dvp)
            for q in range(k + 1, 8):
                m = sb(t[q], k) * rec
                mult[k, q] = m
                t[q] = t[q] - low * m
            if k < 7:
                cur = jnp.where(at & (sub > k), 0.0, cur) - low * sr
        dv[p] = dvp
        n[p] = cur
        inp = (lane >= base) & (lane < base + 8)
        for i in range(p + 1, 16):
            x = [lb(n[i], base + k) for k in range(8)]
            acc = jnp.where(inp, 0.0, n[i])
            for k in range(8):
                for q in range(k + 1, 8):
                    x[q] = x[q] - x[k] * mult[k, q]
                acc = acc - x[k] * rows[k]
            n[i] = acc
    low = []
    for i in range(16):
        r = sub + 8 * i
        low.append(jnp.where(lane < r, n[i], jnp.where(lane == r, 1.0, 0.0)))
    return low, dv

def mm(a, b, ta=False):
    dn = (((0,), (0,)), ((), ())) if ta else (((1,), (0,)), ((), ()))
    return lax.dot_general(a, b, dn, precision=HI, preferred_element_type=F32)


def solve_kernel(alpha, g_ref, d_ref, out_ref, a, bb, li, w, u):
    nb = out_ref.shape[0]
    n = nb * 128
    x = lax.axis_index("mem")
    r = lax.broadcasted_iota(jnp.int32, (128, 128), 0)
    c = lax.broadcasted_iota(jnp.int32, (128, 128), 1)
    for i in range(nb):
        for j in range(i, nb):
            blk = g_ref[pl.ds(16 * i, 16), j].reshape(128, 128)
            a[i, j] = blk + jnp.where(r == c, alpha, 0.0) if i == j else blk
    unit = jnp.where(r == c, alpha * math.sqrt(n - 1.0), 0.0)
    for i in range(nb):
        bb[i] = d_ref[pl.ds(16 * i, 16)].reshape(128, 128) + jnp.where(x == i, unit, 0.0)

    def step(b, _):
        low, dv = factor_block([a[b, b, pl.ds(8 * i, 8), :] for i in range(16)])
        for i in range(16):
            li[b, pl.ds(8 * i, 8), :] = low[i]
            u[pl.ds(8 * i, 8), :] = low[i] * dv[i]
        for s in range(nb):

            @pl.when(b == s)
            def _():
                cols = [a[s, j] for j in range(s + 1, nb)] + [bb[s]]
                us = [mm(li[s], v) for v in cols]
                ws = [mm(u[...], v) for v in cols]
                for t, j in enumerate(range(s + 1, nb)):
                    w[s, j] = ws[t]
                w[s, nb] = ws[-1]
                for t, i in enumerate(range(s + 1, nb)):
                    for q, j in enumerate(range(s + 1, nb)):
                        if j >= i:
                            a[i, j] = a[i, j] - mm(us[t], ws[q], True)
                    bb[i] = bb[i] - mm(us[t], ws[-1], True)

        return 0

    lax.fori_loop(0, nb, step, 0)
    xs = [None] * nb
    for s in reversed(range(nb)):
        acc = w[s, nb]
        for j in range(s + 1, nb):
            acc = acc - mm(w[s, j], xs[j])
        xs[s] = mm(li[s], acc, True)
    tot = sum(jnp.sum(v, axis=0, keepdims=True) for v in xs) * (1.0 / n)
    for s in range(nb):
        out_ref[lax.rem(x + nb - s, nb)] = (xs[s] - tot) * (1.0 / math.sqrt(n - 1.0)) + 1.0 / n


def solve(g, d, alpha):
    nb = g.shape[1]
    block = (128, 128)
    return pl.pallas_call(
        functools.partial(solve_kernel, alpha),
        out_shape=jax.ShapeDtypeStruct((nb, *block), F32),
        in_specs=[VM, VM],
        out_specs=VM,
        scratch_shapes=[
            pltpu.VMEM((nb, nb, *block), F32),
            pltpu.VMEM((nb, *block), F32),
            pltpu.VMEM((nb, *block), F32),
            pltpu.VMEM((nb, nb + 1, *block), F32),
            pltpu.VMEM(block, F32),
        ],
        cost_estimate=pl.CostEstimate(flops=20_000_000_000, bytes_accessed=60_000_000, transcendentals=0),
        name="factor_and_solve",
    )(g, d)


def update_kernel(u_ref, e_ref, l_ref, r_ref, o0_ref, o1_ref, out_ref):
    out_ref[...] = (
        mm(u_ref[0], e_ref[...], True)
        + mm(u_ref[1], l_ref[...].reshape(e_ref.shape), True)
        + mm(u_ref[3], r_ref[...].reshape(e_ref.shape), True)
        + mm(u_ref[2], jnp.concatenate([o0_ref[...], o1_ref[...]], axis=0), True)
    )


def update(u, e, left, right, o0, o1):
    rows, width = e.shape
    t = 512
    return pl.pallas_call(
        update_kernel,
        grid=(width // t,),
        out_shape=jax.ShapeDtypeStruct(e.shape, F32),
        in_specs=[
            pl.BlockSpec(u.shape, lambda i: (0, 0, 0)),
            pl.BlockSpec((rows, t), lambda i: (0, i)),
            pl.BlockSpec((2, rows // 2, t), lambda i: (0, 0, i)),
            pl.BlockSpec((2, rows // 2, t), lambda i: (0, 0, i)),
            pl.BlockSpec((rows // 2, t), lambda i: (0, i)),
            pl.BlockSpec((rows // 2, t), lambda i: (0, i)),
        ],
        out_specs=pl.BlockSpec((rows, t), lambda i: (0, i)),
        name="update",
    )(u, e, left, right, o0, o1)


def shards(ensemble, observed, obs_sigma, obs_index, member_seeds):
    alpha = PLAN[SECTION]
    nx, ny, nz = (lax.axis_size(a) for a in ("mem", "cells_1", "cells_0"))
    own = ensemble.shape[0]
    value = ensemble[:, obs_index]
    predicted = jnp.tanh(value) + 0.5 * value
    seeds = jnp.broadcast_to(member_seeds.astype(F32)[None, :], (8, own))
    pred, all_seeds = exchange(predicted, seeds, nx)
    gp, dp = local_products(pred, all_seeds, observed[None, :], obs_sigma[None, :], nx, alpha)
    tg, td = 256 // (2 * ny * nx), 64 // (2 * ny)
    gp = gp.reshape(2, ny, nx, tg, 8, 128)
    dp = dp.reshape(2, nx, ny, td, 8, 128)
    g, d, left, right = reduce_all(gp, dp, ensemble, nx, ny, nz)
    o0 = lax.ppermute(left[0], "mem", [(i, (i + 1) % nx) for i in range(nx)])
    o1 = lax.ppermute(right[1], "mem", [(i, (i - 1) % nx) for i in range(nx)])
    u = solve(g.reshape(64, 4, 8, 128), d.reshape(64, 8, 128), alpha)
    return update(u, ensemble, left, right, o0, o1)


def solution(mesh):
    finer = Mesh(mesh.devices.reshape(16, 4, 2, mesh.shape["mem"]), AXES)
    placed = (P("mem", CELLS), P(CELLS), P(CELLS), P(CELLS), P("mem"))
    return jax.shard_map(shards, mesh=finer, in_specs=placed, out_specs=P("mem", CELLS), check_vma=False)
```

time: 418 us -> 146 us (0.35); the launches traced: 412 us -> 145 us
  other arithmetic: 132 us -> 2.47 us
  Pallas kernels: 0 us -> 127 us
  waiting for transfers between devices: 95.6 us -> 0.01 us
  blocking collectives: 76 us -> 0 us
  matrix products: 41.9 us -> 0 us
  local copies, waits for them, and re-layouts: 42.6 us -> 10.7 us
  between operations: 16.5 us -> 0.09 us
    pallas_call x0 -> x5, Pallas kernels: none -> 127 us  [the longest x1 68.5 us: reduce_all(): pl.pallas_call(functools.partial(reduce_kernel, (nx, ny, nz)), out_shape=...]
    another operation x18 -> x0, other arithmetic: 125 us -> none  [the longest x15 84.9 us: shards(): jnp.linalg.cholesky(gram_matrix + alpha * jnp.eye(members, dtype=jnp.floa...]
    all_to_all x4 -> x0, blocking collectives: 76 us -> none  [the longest x1 51.2 us: summed_rows(): lax.all_to_all(nearer, far, split_axis=0, concat_axis=0, tiled=True)]
    all_gather x2 -> x0, waiting for transfers between devices: 61.8 us -> none  [the longest x1 61.8 us: shards(): gathered = lax.all_gather(scaled, 'mem', axis=0, tiled=True)]
    all_to_all x1 -> x0, waiting for transfers between devices: 33.7 us -> none  [from_everyone(): return lax.all_to_all(copies, axis, split_axis=0, concat_axis=0, tiled=True)]
    dot_general x3 -> x0, matrix products: 26.8 us -> none  [the longest x1 10.8 us: shards(): jnp.dot(gathered, innovation.T, precision=highest)]
    another operation x35 -> x0, local copies, waits for them, and re-layouts: 17.7 us -> none
    another operation x20 -> x0, matrix products: 15.1 us -> none  [the longest x6 7.86 us: shards(): jnp.linalg.cholesky(gram_matrix + alpha * jnp.eye(members, dtype=jnp.floa...]
  transfers between devices with their start and end apart: 3 -> 2, of which waited for: 2 -> 0; matrix products, arithmetic and copies ran while one was open for 42% -> 0% of each run, Pallas kernels for 0% -> 15%
where the time goes in v1:
time: 146 us; the launch traced here: 145 us
  Pallas kernels  127 us (87%)
  local copies, waits for them, and re-layouts  10.7 us (7%)
  starting transfers between devices  5.46 us (4%)
  other arithmetic  2.47 us (2%)
    pallas_call x1, Pallas kernels, reduce_all(): pl.pallas_call(functools.partial(reduce_kernel, (nx, ny, nz)), out_shape=...  68.5 us
    pallas_call x1, Pallas kernels, solve(): pl.pallas_call(functools.partial(solve_kernel, alpha), out_shape=jax.Shap...  21.9 us
    pallas_call x1, Pallas kernels, exchange(): pl.pallas_call(functools.partial(exchange_kernel, nx), out_shape=(jax.Sha...  17.9 us
    pallas_call x1, Pallas kernels, local_products(): pl.pallas_call(functools.partial(local_kernel, nx, alpha), out_shape=(jax...  11.7 us
    pallas_call x1, Pallas kernels, update(): pl.pallas_call(update_kernel, grid=(width // t,), out_shape=jax.ShapeDtyp...  6.65 us
    gather x2, local copies, waits for them, and re-layouts, shards(): value = ensemble[:, obs_index]  5.8 us
    unnamed x7, local copies, waits for them, and re-layouts  3.12 us
  transfers between devices with their start and end apart: 2, of which 0 were waited for; matrix products, arithmetic and copies ran while one was open for 0% of the time, Pallas kernels for 15%

profile of v1, /device:TPU:1, one launch (start us, length us, event | category | flops | bytes accessed | tf_op | source)
XLA Modules:
  0.0 145.4 jit_solution(11429046866179752704)
XLA Ops:
  0.0 0.7 convert_element_type.3
  0.7 0.7 fusion
  1.4 1.5 %copy.6 = f32[128,2048]{0,1:T(8,128)S(1)} copy(f32[128,2048]{1,0:T(8,128)} %e_ref.3) | data formatting | bytes 2097152 | tf_op args[0]
  2.9 5.5 %gather_fusion = f32[2048,128]{1,0:T(8,128)S(1)} fusion(f32[128,2048]{0,1:T(8,128)S(1)} %copy.6, s32[2048]{0:T(1024)S(1)} %fusion), kind=kCustom, calls=%fused_computation | custom fusion | bytes 2105344 | tf_op jit(solution)/shard_map/gather | solution.py:488
  8.4 0.3 copy.7
  8.7 1.1 add_bitcast_fusion.p_ref
  9.8 0.6 broadcast_in_dim.16.s_ref
  10.4 17.9 %exchange.1 = (f32[512,512]{1,0:T(8,128)}, f32[4,8,128]{2,1,0:T(8,128)}) custom-call(f32[128,2048]{1,0:T(8,128)} %add_bitcast_fusion.p_ref, f32[8,128]{1,0:T(8,128)} %broadcast_in_dim.16.s_ref), custom_call_target="tpu_custom_call" | custom-call | tf_op jit(solution)/shard_map/exchange/pallas_call | solution.py:69
  28.4 11.7 %local_products.1 = (f32[64,4,8,128]{3,2,1,0:T(8,128)}, f32[2,4,32,8,128]{4,3,2,1,0:T(8,128)}) custom-call(f32[512,512]{1,0:T(8,128)} %get-tuple-element.13.p_ref, f32[4,8,128]{2,1,0:T(8,128)} %get-tuple-element.14.s_ref, f32[1,2048]{1,0:T(1,128)} %bitcast.14, f32[1,2048]{1,0:T(1,128)} %bitcast.15), custom_call_target="tpu_custom_call" | custom-call | tf_op jit(solution)/shard_map/local_products/pallas_call | solution.py:145
  40.1 68.5 %reduce_all.1 = (f32[2,4,4,8,1,8,128]{6,5,4,3,2,1,0:T(8,128)}, f32[2,4,8,1,8,128]{5,4,3,2,1,0:T(8,128)}, f32[2,64,2048]{2,1,0:T(8,128)}, f32[2,64,2048]{2,1,0:T(8,128)}) custom-call(f32[2,4,4,8,8,128]{5,4,3,2,1,0:T(8,128)} %bitcast.12, f32[2,4,4,8,8,128]{5,4,3,2,1,0:T(8,128)} %bitcast.13, f32[128,2048]{1,0:T(8,128)} %e_ref.3), custom_call_target="tpu_custom_call" | custom-call | tf_op jit(solution)/shard_map/reduce_all/pallas_call | solution.py:302
  108.6 0.0 copy-start
  108.6 1.2 slice_bitcast_fusion
  109.8 2.8 %collective-permute-start.1 = (f32[64,2048]{1,0:T(8,128)S(1)}, f32[64,2048]{1,0:T(8,128)S(1)}, u32[]{:S(2)}, u32[]{:S(2)}) collective-permute-start(f32[64,2048]{1,0:T(8,128)S(1)} %slice_bitcast_fusion), channel_id=1, source_target_pairs={{0,3},{1,0},{2,1},{3,2},{4,7},{5,4},{6,5},{7,6},{8,11},{9,8},{10,9... | collective-permute-start | bytes 1572872 | tf_op jit(solution)/shard_map/ppermute | solution.py:498
  112.6 0.0 copy-done
  112.6 2.7 %collective-permute-start = (f32[64,2048]{1,0:T(8,128)S(1)}, f32[64,2048]{1,0:T(8,128)S(1)}, u32[]{:S(2)}, u32[]{:S(2)}) collective-permute-start(f32[64,2048]{1,0:T(8,128)S(1)} %slice_bitcast_fusion.1), channel_id=1, source_target_pairs={{0,1},{1,2},{2,3},{3,0},{4,5},{5,6},{6,7},{7,4},{8,9},{9,10},{10,1... | collective-permute-start | bytes 1572872 | tf_op jit(solution)/shard_map/ppermute | solution.py:497
  115.3 21.9 %factor_and_solve.1.u_ref = f32[4,128,128]{2,1,0:T(8,128)} custom-call(f32[64,4,8,128]{3,2,1,0:T(8,128)} %bitcast.16, f32[64,8,128]{2,1,0:T(8,128)} %bitcast.17), custom_call_target="tpu_custom_call" | custom-call | flops 20000000000 | bytes 60000000 | tf_op jit(solution)/shard_map/factor_and_solve/pallas_call | solution.py:438
  137.2 0.0 collective-permute-done.1.o1_ref
  137.2 0.0 copy-start.1
  137.2 0.0 collective-permute-done.o0_ref
  137.2 0.8 copy-done.1
  138.0 0.0 copy-start.2
  138.0 0.8 copy-done.2
  138.8 6.7 %update.1 = f32[128,2048]{1,0:T(8,128)} custom-call(f32[4,128,128]{2,1,0:T(8,128)} %factor_and_solve.1.u_ref, f32[128,2048]{1,0:T(8,128)} %e_ref.3, f32[2,64,2048]{2,1,0:T(8,128)} %get-tuple-element.19.l_ref, f32[2,64,2048]{2,1,0:T(8,128)} %get-tuple-element.20.r_ref, f32[64,2048]{1,0:T(8,128)} %copy-done.2, f32[64,2048]{1,0:T(8,128)} %copy-done.1), custom_call_target="tpu_custom_call" | custom-call | tf_op jit(solution)/shard_map/update/pallas_call | solution.py:467
  (1 shorter events, 0.0 us)
Async XLA Ops:
  108.6 4.0 %copy-start = (f32[2,64,2048]{2,1,0:T(8,128)S(1)}, f32[2,64,2048]{2,1,0:T(8,128)}, u32[]{:S(2)}) copy-start(f32[2,64,2048]{2,1,0:T(8,128)} %get-tuple-element.19.l_ref) | copy-start | bytes 3145732
  109.8 27.4 %collective-permute-start.1 = (f32[64,2048]{1,0:T(8,128)S(1)}, f32[64,2048]{1,0:T(8,128)S(1)}, u32[]{:S(2)}, u32[]{:S(2)}) collective-permute-start(f32[64,2048]{1,0:T(8,128)S(1)} %slice_bitcast_fusion), channel_id=1, source_target_pairs={{0,3},{1,0},{2,1},{3,2},{4,7},{5,4},{6,5},{7,6},{8,11},{9,8},{10,9... | collective-permute-start | bytes 1572872 | tf_op jit(solution)/shard_map/ppermute | solution.py:498
  112.6 24.6 %collective-permute-start = (f32[64,2048]{1,0:T(8,128)S(1)}, f32[64,2048]{1,0:T(8,128)S(1)}, u32[]{:S(2)}, u32[]{:S(2)}) collective-permute-start(f32[64,2048]{1,0:T(8,128)S(1)} %slice_bitcast_fusion.1), channel_id=1, source_target_pairs={{0,1},{1,2},{2,3},{3,0},{4,5},{5,6},{6,7},{7,4},{8,9},{9,10},{10,1... | collective-permute-start | bytes 1572872 | tf_op jit(solution)/shard_map/ppermute | solution.py:497
  137.2 0.8 copy-start.1
  138.0 0.8 copy-start.2

commit v2 on v1

v2 whole, which is shorter than its diff:
```python
import functools
import math

import jax
import jax.numpy as jnp
from jax import lax
from jax.experimental import pallas as pl
from jax.experimental.pallas import tpu as pltpu
from jax.sharding import Mesh
from jax.sharding import PartitionSpec as P

SECTION = 1
CELLS = ("cells_0", "cells_1", "cells_2")
AXES = ("cells_0", "cells_1", "cells_2", "mem")
PLAN = (28.0 / 3.0, 7.0, 4.0, 2.0)
HI = lax.Precision.HIGHEST
BF = jnp.bfloat16
MESH = pl.DeviceIdType.MESH
VM = pl.BlockSpec(memory_space=pltpu.VMEM)
ANY = pl.BlockSpec(memory_space=pl.ANY)
F32 = jnp.float32


def remote(src, dst, send, recv, where):
    return pltpu.make_async_remote_copy(
        src_ref=src, dst_ref=dst, send_sem=send, recv_sem=recv, device_id=where, device_id_type=MESH
    )


def at_axis(axis, index):
    return {axis: index}


def greet(peers):
    barrier = pltpu.get_barrier_semaphore()
    for peer in peers:
        pl.semaphore_signal(barrier, inc=1, device_id=peer, device_id_type=MESH)
    pl.semaphore_wait(barrier, len(peers))


def order_of(n):
    return sorted(range(1, n), key=lambda d: -min(d, n - d))


def mod_prime(v):
    q = jnp.floor(v.astype(F32) * (1.0 / 65521.0)).astype(jnp.int32)
    r = v - q * 65521
    r = jnp.where(r < 0, r + 65521, r)
    return jnp.where(r >= 65521, r - 65521, r)


def cosine(h):
    h = jnp.minimum(h, 65521 - h)
    v = (65521 - 4 * h).astype(F32) * (math.pi / (2.0 * 65521.0))
    s = v * v
    poly = jnp.full_like(s, -1.0 / 39916800.0)
    for k in (9, 7, 5, 3, 1):
        poly = poly * s + (-1.0) ** ((k - 1) // 2) / math.factorial(k)
    return poly * v


def halves(v):
    high = v.astype(BF)
    return high, (v - high.astype(F32)).astype(BF)


def bdot(a, b, dims=((1,), (0,))):
    return lax.dot_general(a, b, (dims, ((), ())), preferred_element_type=F32)


def observe_kernel(nx, alpha, e_ref, i_ref, s_ref, o_ref, n_ref, parts, hot, ready, seeds, send, recv):
    x = lax.axis_index("mem")
    rows, cells = e_ref.shape
    width = i_ref.shape[1] // nx
    barrier = pltpu.get_barrier_semaphore()
    for d in range(1, nx):
        pl.semaphore_signal(barrier, inc=1, device_id={"mem": lax.rem(x + d, nx)}, device_id_type=MESH)
    step = 512

    def split(k, _):
        cols = pl.ds(pl.multiple_of(k * step, step), step)
        v = e_ref[:, cols]
        high, rest = halves(v)
        parts[pl.ds(0, rows), cols] = high
        parts[pl.ds(rows, rows), cols] = rest
        parts[pl.ds(2 * rows, rows), cols] = (v - high.astype(F32) - rest.astype(F32)).astype(BF)
        return 0

    lax.fori_loop(0, cells // step, split, 0)
    lanes = 256
    copies = []
    for d in order_of(nx) + [0]:
        to = lax.rem(x + d, nx)

        def some(h, _):
            index = i_ref[:, pl.ds(pl.multiple_of(to * width + h * lanes, lanes), lanes)]

            def fill(k, _):
                at = pl.multiple_of(k * step, step)
                cell = lax.broadcasted_iota(jnp.int32, (step, lanes), 0) + at
                hot[pl.ds(at, step), :] = jnp.where(cell == index, 1.0, 0.0).astype(BF)
                return 0

            lax.fori_loop(0, cells // step, fill, 0)
            got = bdot(parts[...], hot[...])
            value = got[:rows] + got[rows : 2 * rows] + got[2 * rows :]
            ready[d, :, pl.ds(pl.multiple_of(h * lanes, lanes), lanes)] = jnp.tanh(value) + 0.5 * value
            return 0

        lax.fori_loop(0, width // lanes, some, 0)
        mine = pl.ds(pl.multiple_of(x * rows, rows), rows)
        if not copies:
            pl.semaphore_wait(barrier, nx - 1)
            for k in range(1, nx):
                there = {"mem": lax.rem(x + k, nx)}
                copies.append(remote(s_ref, seeds.at[x], send.at[1, k], recv.at[1, k], there))
                copies[-1].start()
        if d:
            copies.append(remote(ready.at[d], o_ref.at[mine, :], send.at[0, d], recv.at[0, d], {"mem": to}))
            copies[-1].start()
        else:
            o_ref[mine, :] = ready[0]
    seeds[x] = s_ref[...]
    for c in copies[: nx - 1]:
        c.wait_recv()
    base = lax.axis_index(CELLS) * i_ref.shape[1] + x * width
    where = mod_prime(lax.broadcasted_iota(jnp.int32, (1, width), 1) + base)

    def noise(b, _):
        at = pl.ds(pl.multiple_of(b * rows, rows), rows)
        seed = jnp.broadcast_to(seeds[b, 0:1, :], (rows, rows)).T.astype(jnp.int32)
        first = mod_prime(seed * 389)
        second = seed - 997 * jnp.floor((seed.astype(F32) + 0.5) * (1.0 / 997.0)).astype(jnp.int32) + 1
        for c in range(width // 128):
            cols = slice(128 * c, 128 * c + 128)
            n_ref[at, cols] = cosine(mod_prime(first + where[:, cols] * second)) * math.sqrt(2.0 * alpha)
        return 0

    lax.fori_loop(0, nx, noise, 0)
    for c in copies[nx - 1 :]:
        c.wait_recv()
    for c in copies:
        c.wait_send()


def observe(e, index, seeds, nx, alpha):
    rows, cells = e.shape
    width = index.shape[1] // nx
    whole = jax.ShapeDtypeStruct((rows * nx, width), F32)
    return pl.pallas_call(
        functools.partial(observe_kernel, nx, alpha),
        out_shape=(whole, whole),
        in_specs=[VM, VM, VM],
        out_specs=(VM, VM),
        scratch_shapes=[
            pltpu.VMEM((3 * rows, cells), BF),
            pltpu.VMEM((cells, 256), BF),
            pltpu.VMEM((nx, rows, width), F32),
            pltpu.VMEM((nx, 8, rows), F32),
            pltpu.SemaphoreType.DMA((2, nx)),
            pltpu.SemaphoreType.DMA((2, nx)),
        ],
        compiler_params=pltpu.CompilerParams(collective_id=0, has_side_effects=True),
        name="observe",
    )(e, index, seeds)


def product_fills(p_ref, n_ref, ob_ref, sg_ref, gp, dp, sh, sl, mh, ml):
    members, width = p_ref.shape
    blocks = members // 128

    def prepare():
        mean = jnp.sum(p_ref[...], axis=0, keepdims=True) * (1.0 / members)
        part = pl.ds(pl.multiple_of(lax.axis_index("mem") * width, width), width)
        inv = 1.0 / sg_ref[:, part]
        scale = inv * (1.0 / math.sqrt(members - 1.0))
        shift = (ob_ref[:, part] - mean) * inv

        def block(b, _):
            rows = pl.ds(pl.multiple_of(b * 64, 64), 64)
            sh[rows, :], sl[rows, :] = halves((p_ref[rows, :] - mean) * scale)
            mh[rows, :], ml[rows, :] = halves(n_ref[rows, :] + shift)
            return 0

        lax.fori_loop(0, members // 64, block, 0)

    both = ((1,), (1,))

    def fill_d():
        def block(b, _):
            rows = pl.ds(pl.multiple_of(b * 128, 128), 128)
            within = pl.ds(pl.multiple_of(lax.rem(b, 2) * 16, 16), 16)
            d = bdot(sh[rows, :], mh[...], both) + bdot(sh[rows, :], ml[...], both) + bdot(sl[rows, :], mh[...], both)
            for c in range(blocks):
                dp[b // 2, c, within] = d[:, 128 * c : 128 * c + 128].reshape(16, 8, 128)
            return 0

        lax.fori_loop(0, blocks, block, 0)

    def fill_g():
        at = 0
        for b in range(blocks):
            rows, rest = pl.ds(128 * b, 128), pl.ds(128 * b, members - 128 * b)
            g = (
                bdot(sh[rows, :], sh[rest, :], both)
                + bdot(sl[rows, :], sh[rest, :], both)
                + bdot(sh[rows, :], sl[rest, :], both)
                + bdot(sl[rows, :], sl[rest, :], both)
            )
            for c in range(blocks - b):
                gp[pl.ds(at, 16)] = g[:, 128 * c : 128 * c + 128].reshape(16, 8, 128)
                at += 16

    return prepare, fill_d, fill_g


def reduce_kernel(n, fills, n_in, *refs):
    nx, ny, nz = n
    (e_ref, go, do, left, right, opp, gp, dp, rg0, rd0, sg0, sd0, rg1, rd1, sg1, sd1, rg2, rd2, zs, rz, zg,
     cs, cr, xs, xr, ys, yr, zss, zsr, es, er) = refs[n_in : n_in + 31]
    prepare, fill_d, fill_g = fills(*refs[:n_in], gp, dp, *refs[n_in + 31 :])
    z, y, c, x = (lax.axis_index(a) for a in AXES)
    oc = 1 - c

    def xat(d):
        return lax.rem(x + d, nx)

    def yat(d):
        return lax.rem(y + d, ny)

    def zat(d):
        return lax.rem(z + d, nz)

    core = {"cells_2": oc}
    peers = (
        [{"cells_0": zat(d)} for d in range(1, nz)]
        + [{"mem": xat(d)} for d in range(1, nx)]
        + [{"cells_1": yat(d)} for d in range(1, ny)]
        + [core]
    )
    barrier = pltpu.get_barrier_semaphore()
    for peer in peers:
        pl.semaphore_signal(barrier, inc=1, device_id=peer, device_id_type=MESH)
    ox, oy, oz = order_of(nx) + [0], order_of(ny) + [0], order_of(nz)
    sent = []

    def start(copy):
        copy.start()
        sent.append(copy)
        return copy

    prepare()
    fill_d()
    td, tg = rd2.shape[1], rg2.shape[1]
    q = zs.shape[0] // nz

    def g_of(core_, yq):
        return pl.ds((core_ * ny + yq) * nx * tg, nx * tg)

    pl.semaphore_wait(barrier, len(peers))
    c0d, c0g = {}, {}
    for d in ox:
        c0d[d] = start(remote(dp.at[oc, xat(d)], rd0.at[xat(d)], cs.at[0, d], cr.at[0, d], core))
    fill_g()
    for d in oy:
        c0g[d] = start(remote(gp.at[g_of(oc, yat(d))], rg0.at[yat(d)], cs.at[1, d], cr.at[1, d], core))
    d1, g1 = {}, {}
    for d in ox:
        c0d[d].wait_recv()
        sd0[xat(d)] = dp[c, xat(d)] + rd0[xat(d)]
        if d:
            d1[d] = start(remote(sd0.at[xat(d)], rd1.at[d], xs.at[0, d], xr.at[0, d], {"mem": xat(d)}))
    for d in oy:
        c0g[d].wait_recv()
        sg0[yat(d)] = gp[g_of(c, yat(d))] + rg0[yat(d)]
        if d:
            g1[d] = start(remote(sg0.at[yat(d)], rg1.at[d], ys.at[0, d], yr.at[0, d], {"cells_1": yat(d)}))
    d2, g2 = {}, {}
    for d in oy[:-1]:
        g1[d].wait_recv()
    for d in ox:
        piece = pl.ds(xat(d) * tg, tg)
        total = sg0[y, piece]
        for k in range(1, ny):
            total = total + rg1[k, piece]
        sg1[xat(d)] = total
        if d:
            g2[d] = start(remote(sg1.at[xat(d)], rg2.at[d], xs.at[1, d], xr.at[1, d], {"mem": xat(d)}))
    for d in ox[:-1]:
        d1[d].wait_recv()
    for d in oy:
        piece = pl.ds(yat(d) * td, td)
        total = sd0[x, piece]
        for k in range(1, nx):
            total = total + rd1[k, piece]
        sd1[yat(d)] = total
        if d:
            d2[d] = start(remote(sd1.at[yat(d)], rd2.at[d], ys.at[1, d], yr.at[1, d], {"cells_1": yat(d)}))
    half = e_ref.shape[0] // 2
    eo = {}

    def ensemble(h):
        part = e_ref.at[pl.ds(h * half, half), :]
        eo[0, h] = start(remote(part, left.at[h], es.at[0, h], er.at[0, h], {"mem": xat(1)}))
        other = e_ref.at[pl.ds((1 - h) * half, half), :]
        eo[1, h] = start(remote(other, right.at[1 - h], es.at[1, h], er.at[1, h], {"mem": xat(nx - 1)}))

    ensemble(0)
    ensemble(1)
    for t in range(td + tg, nz * q):
        zs[t] = jnp.zeros_like(zs[t])
    for d in ox[:-1]:
        g2[d].wait_recv()
    total = sg1[x]
    for k in range(1, nx):
        total = total + rg2[k]
    zs[pl.ds(td, tg)] = total
    for d in oy[:-1]:
        d2[d].wait_recv()
    total = sd1[y]
    for k in range(1, ny):
        total = total + rd2[k]
    zs[pl.ds(0, td)] = total
    z1 = [
        start(remote(zs.at[pl.ds(zat(d) * q, q)], rz.at[d], zss.at[0, d], zsr.at[0, d], {"cells_0": zat(d)})) for d in oz
    ]
    for w in z1:
        w.wait_recv()
    own = pl.ds(z * q, q)
    total = zs[own]
    for k in range(1, nz):
        total = total + rz[k]
    zg[own] = total
    z2 = [start(remote(zg.at[own], zg.at[own], zss.at[1, d], zsr.at[1, d], {"cells_0": zat(d)})) for d in oz]
    for w in z2:
        w.wait_recv()

    def go_of(yq):
        return pl.ds((c * ny + yq) * nx * tg, nx * tg)

    def do_of(yq):
        return pl.ds((c * ny + yq) * td, td)

    mine = pl.ds(((c * ny + y) * nx + x) * tg, tg)
    go[mine] = zg[pl.ds(td, tg)]
    do[do_of(y)] = zg[pl.ds(0, td)]
    dy, gx, gy = {}, {}, {}
    for d in ox[:-1]:
        gx[d] = start(remote(zg.at[pl.ds(td, tg)], go.at[mine], xs.at[2, d], xr.at[2, d], {"mem": xat(d)}))
    for d in oy[:-1]:
        dy[d] = start(remote(zg.at[pl.ds(0, td)], do.at[do_of(y)], ys.at[2, d], yr.at[2, d], {"cells_1": yat(d)}))
    last = [start(remote(zg.at[pl.ds(0, td)], do.at[do_of(y)], cs.at[2, 0], cr.at[2, 0], core))]
    for d in ox[:-1]:
        gx[d].wait_recv()
    for d in oy[:-1]:
        gy[d] = start(remote(go.at[go_of(y)], go.at[go_of(y)], ys.at[3, d], yr.at[3, d], {"cells_1": yat(d)}))
    last.append(start(remote(go.at[go_of(y)], go.at[go_of(y)], cs.at[3, 0], cr.at[3, 0], core)))
    eo[0, 0].wait_recv()
    eo[1, 0].wait_recv()
    far = [
        start(remote(left.at[0], opp.at[0], es.at[2, 0], er.at[2, 0], {"mem": xat(1)})),
        start(remote(right.at[1], opp.at[1], es.at[2, 1], er.at[2, 1], {"mem": xat(nx - 1)})),
    ]
    for d in sorted(oy[:-1]):
        dy[d].wait_recv()
        frm = do_of(yat(ny - d))
        last.append(start(remote(do.at[frm], do.at[frm], cs.at[2, d], cr.at[2, d], core)))
    for d in reversed(oy[:-1]):
        gy[d].wait_recv()
        frm = go_of(yat(ny - d))
        last.append(start(remote(go.at[frm], go.at[frm], cs.at[3, d], cr.at[3, d], core)))
    for w in last + far + [eo[0, 1], eo[1, 1]]:
        w.wait_recv()
    for w in sent:
        w.wait_send()


def reduce_all(inputs, fills, extra, e, tg, td, nx, ny, nz):
    q = -(-(tg + td) // nz)
    tile = (8, 128)
    m = max(nx, ny)
    half = (2, e.shape[0] // 2, e.shape[1])
    dma = pltpu.SemaphoreType.DMA

    def tiles(*lead):
        return pltpu.VMEM((*lead, *tile), F32)

    return pl.pallas_call(
        functools.partial(reduce_kernel, (nx, ny, nz), fills, len(inputs)),
        out_shape=(
            jax.ShapeDtypeStruct((2 * ny * nx * tg, *tile), F32),
            jax.ShapeDtypeStruct((2 * ny * td, *tile), F32),
            jax.ShapeDtypeStruct(half, F32),
            jax.ShapeDtypeStruct(half, F32),
            jax.ShapeDtypeStruct(half, F32),
        ),
        in_specs=[VM] * len(inputs) + [ANY],
        out_specs=(VM, VM, ANY, ANY, ANY),
        scratch_shapes=[
            tiles(2 * ny * nx * tg),
            tiles(2, nx, ny * td),
            tiles(ny, nx * tg),
            tiles(nx, ny * td),
            tiles(ny, nx * tg),
            tiles(nx, ny * td),
            tiles(ny, nx * tg),
            tiles(nx, ny * td),
            tiles(nx, tg),
            tiles(ny, td),
            tiles(nx, tg),
            tiles(ny, td),
            tiles(nz * q),
            tiles(nz, q),
            tiles(nz * q),
            dma((4, m)), dma((4, m)), dma((3, nx)), dma((3, nx)), dma((4, ny)), dma((4, ny)), dma((2, nz)), dma((2, nz)),
            dma((3, 2)), dma((3, 2)),
            *extra,
        ],
        compiler_params=pltpu.CompilerParams(collective_id=1, has_side_effects=True),
        name="reduce_all",
    )(*inputs, e)


def factor_block(blk):
    lane = lax.broadcasted_iota(jnp.int32, (8, 128), 1)
    sub = lax.broadcasted_iota(jnp.int32, (8, 128), 0)
    n = list(blk)
    dv = [None] * 16
    def lb(x, c):
        return jnp.broadcast_to(x[:, c:c + 1], (8, 128))
    def sb(x, k):
        return jnp.broadcast_to(x[k:k + 1, :], (8, 128))
    for p in range(16):
        base = 8 * p
        t = [lb(n[p], base + k) for k in range(8)]
        mult = {}
        rows = []
        cur = n[p]
        dvp = None
        for k in range(8):
            rec = 1.0 / sb(t[k], k)
            low = jnp.where(sub > k, t[k], 0.0)
            at = lane == base + k
            r = sb(cur, k)
            sr = jnp.where(at, rec, r * rec)
            rows.append(sr if k == 7 else jnp.where((lane > base + k) & (lane < base + 8), 0.0, sr))
            dvp = rec if dvp is None else jnp.where(sub == k, rec, dvp)
            for q in range(k + 1, 8):
                m = sb(t[q], k) * rec
                mult[k, q] = m
                t[q] = t[q] - low * m
            if k < 7:
                cur = jnp.where(at & (sub > k), 0.0, cur) - low * sr
        dv[p] = dvp
        n[p] = cur
        inp = (lane >= base) & (lane < base + 8)
        for i in range(p + 1, 16):
            x = [lb(n[i], base + k) for k in range(8)]
            acc = jnp.where(inp, 0.0, n[i])
            for k in range(8):
                for q in range(k + 1, 8):
                    x[q] = x[q] - x[k] * mult[k, q]
                acc = acc - x[k] * rows[k]
            n[i] = acc
    low = []
    for i in range(16):
        r = sub + 8 * i
        low.append(jnp.where(lane < r, n[i], jnp.where(lane == r, 1.0, 0.0)))
    return low, dv

def mm(a, b, ta=False):
    dn = (((0,), (0,)), ((), ())) if ta else (((1,), (0,)), ((), ()))
    return lax.dot_general(a, b, dn, precision=HI, preferred_element_type=F32)


def solve_kernel(alpha, g_ref, d_ref, out_ref, a, bb, li, w, u):
    nb = out_ref.shape[0]
    n = nb * 128
    first = 0
    x = lax.axis_index("mem")
    r = lax.broadcasted_iota(jnp.int32, (128, 128), 0)
    c = lax.broadcasted_iota(jnp.int32, (128, 128), 1)
    for i in range(nb):
        for j in range(i, nb):
            blk = g_ref[pl.ds(first, 16)].reshape(128, 128)
            first += 16
            a[i, j] = blk + jnp.where(r == c, alpha, 0.0) if i == j else blk
    unit = jnp.where(r == c, alpha * math.sqrt(n - 1.0), 0.0)
    for i in range(nb):
        bb[i] = d_ref[pl.ds(16 * i, 16)].reshape(128, 128) + jnp.where(x == i, unit, 0.0)

    def step(b, _):
        low, dv = factor_block([a[b, b, pl.ds(8 * i, 8), :] for i in range(16)])
        for i in range(16):
            li[b, pl.ds(8 * i, 8), :] = low[i]
            u[pl.ds(8 * i, 8), :] = low[i] * dv[i]
        for s in range(nb):

            @pl.when(b == s)
            def _():
                cols = [a[s, j] for j in range(s + 1, nb)] + [bb[s]]
                us = [mm(li[s], v) for v in cols]
                ws = [mm(u[...], v) for v in cols]
                for t, j in enumerate(range(s + 1, nb)):
                    w[s, j] = ws[t]
                w[s, nb] = ws[-1]
                for t, i in enumerate(range(s + 1, nb)):
                    for q, j in enumerate(range(s + 1, nb)):
                        if j >= i:
                            a[i, j] = a[i, j] - mm(us[t], ws[q], True)
                    bb[i] = bb[i] - mm(us[t], ws[-1], True)

        return 0

    lax.fori_loop(0, nb, step, 0)
    xs = [None] * nb
    for s in reversed(range(nb)):
        acc = w[s, nb]
        for j in range(s + 1, nb):
            acc = acc - mm(w[s, j], xs[j])
        xs[s] = mm(li[s], acc, True)
    tot = sum(jnp.sum(v, axis=0, keepdims=True) for v in xs) * (1.0 / n)
    for s in range(nb):
        out_ref[lax.rem(x + nb - s, nb)] = (xs[s] - tot) * (1.0 / math.sqrt(n - 1.0)) + 1.0 / n


def solve(g, d, alpha):
    nb = d.shape[0] // 16
    block = (128, 128)
    return pl.pallas_call(
        functools.partial(solve_kernel, alpha),
        out_shape=jax.ShapeDtypeStruct((nb, *block), F32),
        in_specs=[VM, VM],
        out_specs=VM,
        scratch_shapes=[
            pltpu.VMEM((nb, nb, *block), F32),
            pltpu.VMEM((nb, *block), F32),
            pltpu.VMEM((nb, *block), F32),
            pltpu.VMEM((nb, nb + 1, *block), F32),
            pltpu.VMEM(block, F32),
        ],
        cost_estimate=pl.CostEstimate(flops=20_000_000_000, bytes_accessed=60_000_000, transcendentals=0),
        name="factor_and_solve",
    )(g, d)


def update_kernel(u_ref, e_ref, l_ref, r_ref, o_ref, out_ref):
    total = None
    for d, ref in ((0, e_ref), (1, l_ref), (2, o_ref), (3, r_ref)):
        uh, ul = halves(u_ref[d])
        eh, el = halves(ref[...].reshape(e_ref.shape))
        for a, b in ((uh, eh), (uh, el), (ul, eh)):
            part = bdot(a, b, ((0,), (0,)))
            total = part if total is None else total + part
    out_ref[...] = total


def update(u, e, left, right, opp):
    rows, width = e.shape
    t = 512
    pair = pl.BlockSpec((2, rows // 2, t), lambda i: (0, 0, i))
    return pl.pallas_call(
        update_kernel,
        grid=(width // t,),
        out_shape=jax.ShapeDtypeStruct(e.shape, F32),
        in_specs=[
            pl.BlockSpec(u.shape, lambda i: (0, 0, 0)),
            pl.BlockSpec((rows, t), lambda i: (0, i)),
            pair,
            pair,
            pair,
        ],
        out_specs=pl.BlockSpec((rows, t), lambda i: (0, i)),
        name="update",
    )(u, e, left, right, opp)


def shards(ensemble, observed, obs_sigma, obs_index, member_seeds):
    alpha = PLAN[SECTION]
    nx, ny, nz = (lax.axis_size(a) for a in ("mem", "cells_1", "cells_0"))
    own = ensemble.shape[0]
    blocks = own * nx // 128
    seeds = jnp.broadcast_to(member_seeds.astype(F32)[None, :], (8, own))
    pred, noise = observe(ensemble, obs_index[None, :], seeds, nx, alpha)
    width = pred.shape[1]
    g, d, left, right, opp = reduce_all(
        (pred, noise, observed[None, :], obs_sigma[None, :]),
        product_fills,
        [pltpu.VMEM((own * nx, width), BF)] * 4,
        ensemble,
        16 * blocks * (blocks + 1) // 2 // (2 * ny * nx),
        16 * blocks // (2 * ny),
        nx,
        ny,
        nz,
    )
    return update(solve(g, d, alpha), ensemble, left, right, opp)


def solution(mesh):
    finer = Mesh(mesh.devices.reshape(16, 4, 2, mesh.shape["mem"]), AXES)
    placed = (P("mem", CELLS), P(CELLS), P(CELLS), P(CELLS), P("mem"))
    return jax.shard_map(shards, mesh=finer, in_specs=placed, out_specs=P("mem", CELLS), check_vma=False)
```

time: 146 us -> 119 us (0.82)
  Pallas kernels: 127 us -> 117 us
  local copies, waits for them, and re-layouts: 10.7 us -> 1.25 us
  starting transfers between devices: 5.46 us -> 0 us
  other arithmetic: 2.47 us -> 0.01 us
    pallas_call x3 -> x2, Pallas kernels: 98.1 us -> 90 us  [the longest x1 71 us: reduce_all(): pl.pallas_call(functools.partial(reduce_kernel, (nx, ny, nz), fills, len(...]
    gather x2 -> x0, local copies, waits for them, and re-layouts: 5.8 us -> none  [shards(): value = ensemble[:, obs_index]]
    ppermute x2 -> x0, starting transfers between devices: 5.46 us -> none  [the longest x1 2.81 us: shards(): o1 = lax.ppermute(right[1], 'mem', [(i, (i - 1) % nx) for i in range(nx)])]
    unnamed x7 -> x2, local copies, waits for them, and re-layouts: 3.12 us -> 0.65 us
  transfers between devices with their start and end apart: 2 -> 0, of which waited for: 0 -> 0; matrix products, arithmetic and copies ran while one was open for 0% -> 0% of each run, Pallas kernels for 15% -> 0%
where the time goes in v2:
time: 119 us; the launch traced here: 118 us
  Pallas kernels  117 us (98%)
  local copies, waits for them, and re-layouts  1.25 us (1%)
    pallas_call x1, Pallas kernels, reduce_all(): pl.pallas_call(functools.partial(reduce_kernel, (nx, ny, nz), fills, len(...  71 us
    pallas_call x1, Pallas kernels, solve(): pl.pallas_call(functools.partial(solve_kernel, alpha), out_shape=jax.Shap...  21.8 us
    pallas_call x1, Pallas kernels, observe(): pl.pallas_call(functools.partial(observe_kernel, nx, alpha), out_shape=(w...  19.1 us
    pallas_call x1, Pallas kernels, update(): pl.pallas_call(update_kernel, grid=(width // t,), out_shape=jax.ShapeDtyp...  5.26 us

profile of v2, /device:TPU:1, one launch (start us, length us, event | category | flops | bytes accessed | tf_op | source)
XLA Modules:
  0.0 118.3 jit_solution(17628675373106253246)
XLA Ops:
  0.0 0.0 copy-start
  0.0 0.7 copy-done
  0.7 0.6 broadcast_in_dim.16.s_ref
  1.3 19.1 %observe.1 = (f32[512,512]{1,0:T(8,128)}, f32[512,512]{1,0:T(8,128)}) custom-call(f32[128,2048]{1,0:T(8,128)} %e_ref.3, s32[1,2048]{1,0:T(1,128)} %bitcast.3, f32[8,128]{1,0:T(8,128)} %broadcast_in_dim.16.s_ref), custom_call_target="tpu_custom_call" | custom-call | tf_op jit(solution)/shard_map/observe/pallas_call | solution.py:150
  20.3 71.0 %reduce_all.1 = (f32[160,8,128]{2,1,0:T(8,128)}, f32[64,8,128]{2,1,0:T(8,128)}, f32[2,64,2048]{2,1,0:T(8,128)}, f32[2,64,2048]{2,1,0:T(8,128)}, f32[2,64,2048]{2,1,0:T(8,128)}) custom-call(f32[512,512]{1,0:T(8,128)} %get-tuple-element.12.refs_0_, f32[512,512]{1,0:T(8,128)} %get-tuple-element.13.refs_1_, f32[1,2048]{1,0:T(1,128)} %bitcast.4, ...), custom_call_target="tpu_custom_call" | custom-call | tf_op jit(solution)/shard_map/reduce_all/pallas_call | solution.py:388
  91.3 21.8 %factor_and_solve.1.u_ref = f32[4,128,128]{2,1,0:T(8,128)} custom-call(f32[160,8,128]{2,1,0:T(8,128)} %get-tuple-element.14.g_ref, f32[64,8,128]{2,1,0:T(8,128)} %get-tuple-element.15.d_ref), custom_call_target="tpu_custom_call" | custom-call | flops 20000000000 | bytes 60000000 | tf_op jit(solution)/shard_map/factor_and_solve/pallas_call | solution.py:530
  113.1 5.3 %update.1 = f32[128,2048]{1,0:T(8,128)} custom-call(f32[4,128,128]{2,1,0:T(8,128)} %factor_and_solve.1.u_ref, f32[128,2048]{1,0:T(8,128)} %e_ref.3, f32[2,64,2048]{2,1,0:T(8,128)} %get-tuple-element.16.l_ref, f32[2,64,2048]{2,1,0:T(8,128)} %get-tuple-element.17.r_ref, f32[2,64,2048]{2,1,0:T(8,128)} %get-tuple-element.18.o_ref), custom_call_target="tpu_custom_call" | custom-call | tf_op jit(solution)/shard_map/update/pallas_call | solution.py:562
  (1 shorter events, 0.0 us)
Async XLA Ops:
  0.0 0.7 copy-start

commit v3 on v2

--- a/solution.py
+++ b/solution.py
@@ -68,28 +68,25 @@
     return lax.dot_general(a, b, (dims, ((), ())), preferred_element_type=F32)
 
 
-def observe_kernel(nx, alpha, e_ref, i_ref, s_ref, o_ref, n_ref, parts, hot, ready, seeds, send, recv):
+def observe_stages(nx, alpha, e_ref, i_ref, s_ref, o_ref, n_ref, parts, hot, ready, seeds, send, recv):
     x = lax.axis_index("mem")
     rows, cells = e_ref.shape
     width = i_ref.shape[1] // nx
-    barrier = pltpu.get_barrier_semaphore()
-    for d in range(1, nx):
-        pl.semaphore_signal(barrier, inc=1, device_id={"mem": lax.rem(x + d, nx)}, device_id_type=MESH)
-    step = 512
-
-    def split(k, _):
-        cols = pl.ds(pl.multiple_of(k * step, step), step)
-        v = e_ref[:, cols]
-        high, rest = halves(v)
-        parts[pl.ds(0, rows), cols] = high
-        parts[pl.ds(rows, rows), cols] = rest
-        parts[pl.ds(2 * rows, rows), cols] = (v - high.astype(F32) - rest.astype(F32)).astype(BF)
-        return 0
-
-    lax.fori_loop(0, cells // step, split, 0)
-    lanes = 256
-    copies = []
-    for d in order_of(nx) + [0]:
+    step, lanes = 512, 256
+
+    def split():
+        def block(k, _):
+            cols = pl.ds(pl.multiple_of(k * step, step), step)
+            v = e_ref[:, cols]
+            high, rest = halves(v)
+            parts[pl.ds(0, rows), cols] = high
+            parts[pl.ds(rows, rows), cols] = rest
+            parts[pl.ds(2 * rows, rows), cols] = (v - high.astype(F32) - rest.astype(F32)).astype(BF)
+            return 0
+
+        lax.fori_loop(0, cells // step, block, 0)
+
+    def predict(d):
         to = lax.rem(x + d, nx)
 
         def some(h, _):
@@ -108,61 +105,37 @@
             return 0
 
         lax.fori_loop(0, width // lanes, some, 0)
+
+    def copies():
         mine = pl.ds(pl.multiple_of(x * rows, rows), rows)
-        if not copies:
-            pl.semaphore_wait(barrier, nx - 1)
-            for k in range(1, nx):
-                there = {"mem": lax.rem(x + k, nx)}
-                copies.append(remote(s_ref, seeds.at[x], send.at[1, k], recv.at[1, k], there))
-                copies[-1].start()
-        if d:
-            copies.append(remote(ready.at[d], o_ref.at[mine, :], send.at[0, d], recv.at[0, d], {"mem": to}))
-            copies[-1].start()
-        else:
-            o_ref[mine, :] = ready[0]
-    seeds[x] = s_ref[...]
-    for c in copies[: nx - 1]:
-        c.wait_recv()
-    base = lax.axis_index(CELLS) * i_ref.shape[1] + x * width
-    where = mod_prime(lax.broadcasted_iota(jnp.int32, (1, width), 1) + base)
-
-    def noise(b, _):
-        at = pl.ds(pl.multiple_of(b * rows, rows), rows)
-        seed = jnp.broadcast_to(seeds[b, 0:1, :], (rows, rows)).T.astype(jnp.int32)
-        first = mod_prime(seed * 389)
-        second = seed - 997 * jnp.floor((seed.astype(F32) + 0.5) * (1.0 / 997.0)).astype(jnp.int32) + 1
-        for c in range(width // 128):
-            cols = slice(128 * c, 128 * c + 128)
-            n_ref[at, cols] = cosine(mod_prime(first + where[:, cols] * second)) * math.sqrt(2.0 * alpha)
-        return 0
-
-    lax.fori_loop(0, nx, noise, 0)
-    for c in copies[nx - 1 :]:
-        c.wait_recv()
-    for c in copies:
-        c.wait_send()
-
-
-def observe(e, index, seeds, nx, alpha):
-    rows, cells = e.shape
-    width = index.shape[1] // nx
-    whole = jax.ShapeDtypeStruct((rows * nx, width), F32)
-    return pl.pallas_call(
-        functools.partial(observe_kernel, nx, alpha),
-        out_shape=(whole, whole),
-        in_specs=[VM, VM, VM],
-        out_specs=(VM, VM),
-        scratch_shapes=[
-            pltpu.VMEM((3 * rows, cells), BF),
-            pltpu.VMEM((cells, 256), BF),
-            pltpu.VMEM((nx, rows, width), F32),
-            pltpu.VMEM((nx, 8, rows), F32),
-            pltpu.SemaphoreType.DMA((2, nx)),
-            pltpu.SemaphoreType.DMA((2, nx)),
-        ],
-        compiler_params=pltpu.CompilerParams(collective_id=0, has_side_effects=True),
-        name="observe",
-    )(e, index, seeds)
+        s, p = [], []
+        for d in order_of(nx):
+            there = {"mem": lax.rem(x + d, nx)}
+            s.append(remote(s_ref, seeds.at[x], send.at[1, d], recv.at[1, d], there))
+            p.append(remote(ready.at[d], o_ref.at[mine, :], send.at[0, d], recv.at[0, d], there))
+        return s, p
+
+    def keep():
+        o_ref[pl.ds(pl.multiple_of(x * rows, rows), rows), :] = ready[0]
+        seeds[x] = s_ref[...]
+
+    def noise():
+        base = lax.axis_index(CELLS) * i_ref.shape[1] + x * width
+        where = mod_prime(lax.broadcasted_iota(jnp.int32, (1, width), 1) + base)
+
+        def block(b, _):
+            at = pl.ds(pl.multiple_of(b * rows, rows), rows)
+            seed = jnp.broadcast_to(seeds[b, 0:1, :], (rows, rows)).T.astype(jnp.int32)
+            first = mod_prime(seed * 389)
+            second = seed - 997 * jnp.floor((seed.astype(F32) + 0.5) * (1.0 / 997.0)).astype(jnp.int32) + 1
+            for c in range(width // 128):
+                cols = slice(128 * c, 128 * c + 128)
+                n_ref[at, cols] = cosine(mod_prime(first + where[:, cols] * second)) * math.sqrt(2.0 * alpha)
+            return 0
+
+        lax.fori_loop(0, nx, block, 0)
+
+    return split, predict, copies, keep, noise
 
 
 def product_fills(p_ref, n_ref, ob_ref, sg_ref, gp, dp, sh, sl, mh, ml):
@@ -214,11 +187,34 @@
     return prepare, fill_d, fill_g
 
 
+def all_fills(nx, alpha):
+    def fills(e_ref, i_ref, s_ref, ob_ref, sg_ref, gp, dp, pred, noi, parts, hot, ready, seeds, send, recv, *split):
+        stages = observe_stages(nx, alpha, e_ref, i_ref, s_ref, pred, noi, parts, hot, ready, seeds, send, recv)
+        return stages, product_fills(pred, noi, ob_ref, sg_ref, gp, dp, *split)
+
+    return fills
+
+
+def all_scratch(rows, cells, width, nx):
+    dma = pltpu.SemaphoreType.DMA
+    whole = (rows * nx, width)
+    return [
+        pltpu.VMEM(whole, F32),
+        pltpu.VMEM(whole, F32),
+        pltpu.VMEM((3 * rows, cells), BF),
+        pltpu.VMEM((cells, 256), BF),
+        pltpu.VMEM((nx, rows, width), F32),
+        pltpu.VMEM((nx, 8, rows), F32),
+        dma((2, nx)),
+        dma((2, nx)),
+    ] + [pltpu.VMEM(whole, BF)] * 4
+
+
 def reduce_kernel(n, fills, n_in, *refs):
     nx, ny, nz = n
     (e_ref, go, do, left, right, opp, gp, dp, rg0, rd0, sg0, sd0, rg1, rd1, sg1, sd1, rg2, rd2, zs, rz, zg,
      cs, cr, xs, xr, ys, yr, zss, zsr, es, er) = refs[n_in : n_in + 31]
-    prepare, fill_d, fill_g = fills(*refs[:n_in], gp, dp, *refs[n_in + 31 :])
+    stages, (prepare, fill_d, fill_g) = fills(*refs[:n_in], gp, dp, *refs[n_in + 31 :])
     z, y, c, x = (lax.axis_index(a) for a in AXES)
     oc = 1 - c
 
@@ -249,15 +245,39 @@
         sent.append(copy)
         return copy
 
+    td, tg = rd2.shape[1], rg2.shape[1]
+    q = zs.shape[0] // nz
+
+    def g_of(core_, yq):
+        return pl.ds((core_ * ny + yq) * nx * tg, nx * tg)
+
+    half = e_ref.shape[0] // 2
+    eo = {}
+
+    def ensemble(h):
+        part = e_ref.at[pl.ds(h * half, half), :]
+        eo[0, h] = start(remote(part, left.at[h], es.at[0, h], er.at[0, h], {"mem": xat(1)}))
+        other = e_ref.at[pl.ds((1 - h) * half, half), :]
+        eo[1, h] = start(remote(other, right.at[1 - h], es.at[1, h], er.at[1, h], {"mem": xat(nx - 1)}))
+
+    split, predict, copies, keep, noise = stages
+    split()
+    for d in ox[:-1]:
+        predict(d)
+    of_seeds, of_pred = copies()
+    pl.semaphore_wait(barrier, len(peers))
+    for w in of_seeds + of_pred:
+        start(w)
+    ensemble(0)
+    predict(0)
+    keep()
+    for w in of_seeds:
+        w.wait_recv()
+    noise()
+    for w in of_pred:
+        w.wait_recv()
     prepare()
     fill_d()
-    td, tg = rd2.shape[1], rg2.shape[1]
-    q = zs.shape[0] // nz
-
-    def g_of(core_, yq):
-        return pl.ds((core_ * ny + yq) * nx * tg, nx * tg)
-
-    pl.semaphore_wait(barrier, len(peers))
     c0d, c0g = {}, {}
     for d in ox:
         c0d[d] = start(remote(dp.at[oc, xat(d)], rd0.at[xat(d)], cs.at[0, d], cr.at[0, d], core))
@@ -296,16 +316,6 @@
         sd1[yat(d)] = total
         if d:
             d2[d] = start(remote(sd1.at[yat(d)], rd2.at[d], ys.at[1, d], yr.at[1, d], {"cells_1": yat(d)}))
-    half = e_ref.shape[0] // 2
-    eo = {}
-
-    def ensemble(h):
-        part = e_ref.at[pl.ds(h * half, half), :]
-        eo[0, h] = start(remote(part, left.at[h], es.at[0, h], er.at[0, h], {"mem": xat(1)}))
-        other = e_ref.at[pl.ds((1 - h) * half, half), :]
-        eo[1, h] = start(remote(other, right.at[1 - h], es.at[1, h], er.at[1, h], {"mem": xat(nx - 1)}))
-
-    ensemble(0)
     ensemble(1)
     for t in range(td + tg, nz * q):
         zs[t] = jnp.zeros_like(zs[t])
@@ -421,59 +431,69 @@
     )(*inputs, e)
 
 
-def factor_block(blk):
+def factor_block(n_ref, low_ref, solved_ref, zero, span=4):
     lane = lax.broadcasted_iota(jnp.int32, (8, 128), 1)
     sub = lax.broadcasted_iota(jnp.int32, (8, 128), 0)
-    n = list(blk)
-    dv = [None] * 16
-    def lb(x, c):
-        return jnp.broadcast_to(x[:, c:c + 1], (8, 128))
-    def sb(x, k):
-        return jnp.broadcast_to(x[k:k + 1, :], (8, 128))
-    for p in range(16):
-        base = 8 * p
-        t = [lb(n[p], base + k) for k in range(8)]
-        mult = {}
-        rows = []
-        cur = n[p]
-        dvp = None
-        for k in range(8):
-            rec = 1.0 / sb(t[k], k)
-            low = jnp.where(sub > k, t[k], 0.0)
-            at = lane == base + k
-            r = sb(cur, k)
-            sr = jnp.where(at, rec, r * rec)
-            rows.append(sr if k == 7 else jnp.where((lane > base + k) & (lane < base + 8), 0.0, sr))
-            dvp = rec if dvp is None else jnp.where(sub == k, rec, dvp)
-            for q in range(k + 1, 8):
-                m = sb(t[q], k) * rec
-                mult[k, q] = m
-                t[q] = t[q] - low * m
-            if k < 7:
-                cur = jnp.where(at & (sub > k), 0.0, cur) - low * sr
-        dv[p] = dvp
-        n[p] = cur
-        inp = (lane >= base) & (lane < base + 8)
-        for i in range(p + 1, 16):
-            x = [lb(n[i], base + k) for k in range(8)]
-            acc = jnp.where(inp, 0.0, n[i])
-            for k in range(8):
-                for q in range(k + 1, 8):
-                    x[q] = x[q] - x[k] * mult[k, q]
-                acc = acc - x[k] * rows[k]
-            n[i] = acc
-    low = []
-    for i in range(16):
-        r = sub + 8 * i
-        low.append(jnp.where(lane < r, n[i], jnp.where(lane == r, 1.0, 0.0)))
-    return low, dv
+
+    def lb(v, c):
+        return jnp.broadcast_to(v[:, c : c + 1], (8, 128))
+
+    def sb(v, k):
+        return jnp.broadcast_to(v[k : k + 1, :], (8, 128))
+
+    for first in range(0, 16, span):
+        end = 8 * (first + span)
+        n = {i: n_ref[pl.ds(8 * i, 8), :] for i in range(first, first + span)}
+        before, after = [], []
+        for p in range(first, first + span):
+            base = 8 * p
+            cur = n[p]
+            before.append(jnp.where(lane >= end, cur, 0.0))
+            low_ref[pl.ds(base, 8), :] = jnp.where(lane < base, cur, jnp.where(lane == base + sub, 1.0, 0.0))
+            t = [lb(cur, base + k) + zero for k in range(8)]
+            for k in range(0, 8, 2):
+                t0, t1 = t[k], t[k + 1]
+                aa, ab, bb = sb(t0, k), sb(t1, k), sb(t1, k + 1)
+                rec = 1.0 / (aa * bb - ab * ab)
+                pair = (sub == k) | (sub == k + 1)
+                top = sub == k
+                x0, x1 = jnp.where(pair, 0.0, t0), jnp.where(pair, 0.0, t1)
+                s0, s1 = lane == base + k, lane == base + k + 1
+                r0 = jnp.where(s0, 1.0, jnp.where(s1, 0.0, sb(cur, k)))
+                r1 = jnp.where(s1, 1.0, jnp.where(s0, 0.0, sb(cur, k + 1)))
+                n0, n1 = bb * r0 - ab * r1, aa * r1 - ab * r0
+                cur = jnp.where(pair, 0.0, jnp.where(s0 | s1, 0.0, cur)) - jnp.where(
+                    pair, -jnp.where(top, n0, n1), x0 * n0 + x1 * n1
+                ) * rec
+                for q in range(k + 2, 8):
+                    r0, r1 = sb(t[q], k), sb(t[q], k + 1)
+                    n0, n1 = bb * r0 - ab * r1, aa * r1 - ab * r0
+                    t[q] = jnp.where(pair, 0.0, t[q]) - jnp.where(pair, -jnp.where(top, n0, n1), x0 * n0 + x1 * n1) * rec
+            solved_ref[pl.ds(base, 8), :] = jnp.where(lane < base + 8, cur, 0.0)
+            after.append(jnp.where((lane >= base + 8) & (lane < end), 0.0, cur))
+            rows = [sb(cur, k) for k in range(8)]
+            inside = (lane >= base) & (lane < base + 8)
+            for i in range(p + 1, first + span):
+                acc = jnp.where(inside, 0.0, n[i])
+                for k in range(8):
+                    acc = acc - lb(n[i], base + k) * rows[k]
+                n[i] = acc
+        if end < 128:
+            b = jnp.concatenate(before, axis=0)
+            f = jnp.concatenate(after, axis=0)
+            change = lax.dot_general(b, f, (((0,), (0,)), ((), ())), precision=HI, preferred_element_type=jnp.float32)
+            keep = (lane < 8 * first) | (lane >= end)
+            for i in range(first + span, 16):
+                at = pl.ds(8 * i, 8)
+                n_ref[at, :] = jnp.where(keep, n_ref[at, :], 0.0) - change[8 * i : 8 * i + 8]
 
 def mm(a, b, ta=False):
     dn = (((0,), (0,)), ((), ())) if ta else (((1,), (0,)), ((), ()))
     return lax.dot_general(a, b, dn, precision=HI, preferred_element_type=F32)
 
 
-def solve_kernel(alpha, g_ref, d_ref, out_ref, a, bb, li, w, u):
+def solve_kernel(alpha, g_ref, d_ref, out_ref, a, bb, li, w, u, zero):
+    zero[...] = jnp.zeros_like(zero)
     nb = out_ref.shape[0]
     n = nb * 128
     first = 0
@@ -490,10 +510,7 @@
         bb[i] = d_ref[pl.ds(16 * i, 16)].reshape(128, 128) + jnp.where(x == i, unit, 0.0)
 
     def step(b, _):
-        low, dv = factor_block([a[b, b, pl.ds(8 * i, 8), :] for i in range(16)])
-        for i in range(16):
-            li[b, pl.ds(8 * i, 8), :] = low[i]
-            u[pl.ds(8 * i, 8), :] = low[i] * dv[i]
+        factor_block(a.at[b, b], li.at[b], u, zero[...])
         for s in range(nb):
 
             @pl.when(b == s)
@@ -538,6 +555,7 @@
             pltpu.VMEM((nb, *block), F32),
             pltpu.VMEM((nb, nb + 1, *block), F32),
             pltpu.VMEM(block, F32),
+            pltpu.VMEM((8, 128), F32),
         ],
         cost_estimate=pl.CostEstimate(flops=20_000_000_000, bytes_accessed=60_000_000, transcendentals=0),
         name="factor_and_solve",
@@ -580,13 +598,12 @@
     nx, ny, nz = (lax.axis_size(a) for a in ("mem", "cells_1", "cells_0"))
     own = ensemble.shape[0]
     blocks = own * nx // 128
+    width = obs_index.shape[0] // nx
     seeds = jnp.broadcast_to(member_seeds.astype(F32)[None, :], (8, own))
-    pred, noise = observe(ensemble, obs_index[None, :], seeds, nx, alpha)
-    width = pred.shape[1]
     g, d, left, right, opp = reduce_all(
-        (pred, noise, observed[None, :], obs_sigma[None, :]),
-        product_fills,
-        [pltpu.VMEM((own * nx, width), BF)] * 4,
+        (ensemble, obs_index[None, :], seeds, observed[None, :], obs_sigma[None, :]),
+        all_fills(nx, alpha),
+        all_scratch(own, ensemble.shape[1], width, nx),
         ensemble,
         16 * blocks * (blocks + 1) // 2 // (2 * ny * nx),
         16 * blocks // (2 * ny),

time: 119 us -> 108 us (0.908)
  the two profiles are of different devices: /device:TPU:1 before, /device:TPU:32 now
where the time goes in v3:
time: 108 us
  Pallas kernels  107 us (99%)
  local copies, waits for them, and re-layouts  1.25 us (1%)
    pallas_call x1, Pallas kernels, reduce_all(): pl.pallas_call(functools.partial(reduce_kernel, (nx, ny, nz), fills, len(...  82.8 us
    pallas_call x1, Pallas kernels, solve(): pl.pallas_call(functools.partial(solve_kernel, alpha), out_shape=jax.Shap...  18.8 us
    pallas_call x1, Pallas kernels, update(): pl.pallas_call(update_kernel, grid=(width // t,), out_shape=jax.ShapeDtyp...  5.25 us

profile of v3, /device:TPU:32, one launch (start us, length us, event | category | flops | bytes accessed | tf_op | source)
XLA Modules:
  0.0 108.1 jit_solution(11697492134973221788)
XLA Ops:
  0.0 0.0 copy-start
  0.0 0.7 copy-done
  0.7 0.6 broadcast_in_dim.16.refs_2_
  1.3 82.8 %reduce_all.1 = (f32[160,8,128]{2,1,0:T(8,128)}, f32[64,8,128]{2,1,0:T(8,128)}, f32[2,64,2048]{2,1,0:T(8,128)}, f32[2,64,2048]{2,1,0:T(8,128)}, f32[2,64,2048]{2,1,0:T(8,128)}) custom-call(f32[128,2048]{1,0:T(8,128)} %e_ref.1, s32[1,2048]{1,0:T(1,128)} %bitcast.3, f32[8,128]{1,0:T(8,128)} %broadcast_in_dim.16.refs_2_, f32[1,2048]{1,0:T(1,128)} %bitcast.4, ...), custom_call_target="tpu_custom_call" | custom-call | tf_op jit(solution)/shard_map/reduce_all/pallas_call | solution.py:398
  84.1 18.8 %factor_and_solve.1.u_ref = f32[4,128,128]{2,1,0:T(8,128)} custom-call(f32[160,8,128]{2,1,0:T(8,128)} %get-tuple-element.10.g_ref, f32[64,8,128]{2,1,0:T(8,128)} %get-tuple-element.11.d_ref), custom_call_target="tpu_custom_call" | custom-call | flops 20000000000 | bytes 60000000 | tf_op jit(solution)/shard_map/factor_and_solve/pallas_call | solution.py:547
  102.9 5.3 %update.1 = f32[128,2048]{1,0:T(8,128)} custom-call(f32[4,128,128]{2,1,0:T(8,128)} %factor_and_solve.1.u_ref, f32[128,2048]{1,0:T(8,128)} %e_ref.1, f32[2,64,2048]{2,1,0:T(8,128)} %get-tuple-element.12.l_ref, f32[2,64,2048]{2,1,0:T(8,128)} %get-tuple-element.13.r_ref, f32[2,64,2048]{2,1,0:T(8,128)} %get-tuple-element.14.o_ref), custom_call_target="tpu_custom_call" | custom-call | tf_op jit(solution)/shard_map/update/pallas_call | solution.py:580
  (1 shorter events, 0.0 us)
Async XLA Ops:
  0.0 0.7 copy-start

commit v4 on v3

--- a/solution.py
+++ b/solution.py
@@ -68,13 +68,15 @@
     return lax.dot_general(a, b, (dims, ((), ())), preferred_element_type=F32)
 
 
-def observe_stages(nx, alpha, e_ref, i_ref, s_ref, o_ref, n_ref, parts, hot, ready, seeds, send, recv):
+def observe_stages(nx, alpha, e_ref, i_ref, s_ref, o_ref, n_ref, parts, hot, ready, mine_s, seeds, send, recv):
     x = lax.axis_index("mem")
     rows, cells = e_ref.shape
     width = i_ref.shape[1] // nx
     step, lanes = 512, 256
 
     def split():
+        mine_s[...] = jnp.broadcast_to(s_ref[0:1, :].astype(F32), mine_s.shape)
+
         def block(k, _):
             cols = pl.ds(pl.multiple_of(k * step, step), step)
             v = e_ref[:, cols]
@@ -111,13 +113,13 @@
         s, p = [], []
         for d in order_of(nx):
             there = {"mem": lax.rem(x + d, nx)}
-            s.append(remote(s_ref, seeds.at[x], send.at[1, d], recv.at[1, d], there))
+            s.append(remote(mine_s, seeds.at[x], send.at[1, d], recv.at[1, d], there))
             p.append(remote(ready.at[d], o_ref.at[mine, :], send.at[0, d], recv.at[0, d], there))
         return s, p
 
     def keep():
         o_ref[pl.ds(pl.multiple_of(x * rows, rows), rows), :] = ready[0]
-        seeds[x] = s_ref[...]
+        seeds[x] = mine_s[...]
 
     def noise():
         base = lax.axis_index(CELLS) * i_ref.shape[1] + x * width
@@ -188,8 +190,8 @@
 
 
 def all_fills(nx, alpha):
-    def fills(e_ref, i_ref, s_ref, ob_ref, sg_ref, gp, dp, pred, noi, parts, hot, ready, seeds, send, recv, *split):
-        stages = observe_stages(nx, alpha, e_ref, i_ref, s_ref, pred, noi, parts, hot, ready, seeds, send, recv)
+    def fills(e_ref, i_ref, s_ref, ob_ref, sg_ref, gp, dp, pred, noi, parts, hot, ready, mine_s, seeds, send, recv, *split):
+        stages = observe_stages(nx, alpha, e_ref, i_ref, s_ref, pred, noi, parts, hot, ready, mine_s, seeds, send, recv)
         return stages, product_fills(pred, noi, ob_ref, sg_ref, gp, dp, *split)
 
     return fills
@@ -204,6 +206,7 @@
         pltpu.VMEM((3 * rows, cells), BF),
         pltpu.VMEM((cells, 256), BF),
         pltpu.VMEM((nx, rows, width), F32),
+        pltpu.VMEM((8, rows), F32),
         pltpu.VMEM((nx, 8, rows), F32),
         dma((2, nx)),
         dma((2, nx)),
@@ -213,8 +216,8 @@
 def reduce_kernel(n, fills, n_in, *refs):
     nx, ny, nz = n
     (e_ref, go, do, left, right, opp, gp, dp, rg0, rd0, sg0, sd0, rg1, rd1, sg1, sd1, rg2, rd2, zs, rz, zg,
-     cs, cr, xs, xr, ys, yr, zss, zsr, es, er) = refs[n_in : n_in + 31]
-    stages, (prepare, fill_d, fill_g) = fills(*refs[:n_in], gp, dp, *refs[n_in + 31 :])
+     cs, cr, xs, xr, ys, yr, zss, zsr, es, er, heard) = refs[n_in : n_in + 32]
+    stages, (prepare, fill_d, fill_g) = fills(*refs[:n_in], gp, dp, *refs[n_in + 32 :])
     z, y, c, x = (lax.axis_index(a) for a in AXES)
     oc = 1 - c
 
@@ -228,15 +231,22 @@
         return lax.rem(z + d, nz)
 
     core = {"cells_2": oc}
+    beside = [{"cells_0": zat(d)} for d in sorted({1, nz - 1} - {0})] if nz > 1 else []
     peers = (
-        [{"cells_0": zat(d)} for d in range(1, nz)]
-        + [{"mem": xat(d)} for d in range(1, nx)]
-        + [{"cells_1": yat(d)} for d in range(1, ny)]
-        + [core]
+        [{"mem": xat(d)} for d in range(1, nx)] + [{"cells_1": yat(d)} for d in range(1, ny)] + [core] + beside
     )
     barrier = pltpu.get_barrier_semaphore()
     for peer in peers:
         pl.semaphore_signal(barrier, inc=1, device_id=peer, device_id_type=MESH)
+    rounds = list(range(nz // 2 - 1))
+
+    def spread(count=1):
+        for r in rounds[:count]:
+            for peer in beside:
+                pl.semaphore_signal(heard.at[r], inc=1, device_id=peer, device_id_type=MESH)
+            pl.semaphore_wait(heard.at[r], len(beside))
+        del rounds[:count]
+
     ox, oy, oz = order_of(nx) + [0], order_of(ny) + [0], order_of(nz)
     sent = []
 
@@ -269,14 +279,20 @@
     for w in of_seeds + of_pred:
         start(w)
     ensemble(0)
+    spread()
     predict(0)
+    spread()
     keep()
     for w in of_seeds:
         w.wait_recv()
+    spread()
     noise()
+    spread()
     for w in of_pred:
         w.wait_recv()
+        spread()
     prepare()
+    spread(nz)
     fill_d()
     c0d, c0g = {}, {}
     for d in ox:
@@ -423,7 +439,7 @@
             tiles(nz, q),
             tiles(nz * q),
             dma((4, m)), dma((4, m)), dma((3, nx)), dma((3, nx)), dma((4, ny)), dma((4, ny)), dma((2, nz)), dma((2, nz)),
-            dma((3, 2)), dma((3, 2)),
+            dma((3, 2)), dma((3, 2)), pltpu.SemaphoreType.REGULAR((max(nz // 2 - 1, 1),)),
             *extra,
         ],
         compiler_params=pltpu.CompilerParams(collective_id=1, has_side_effects=True),
@@ -492,105 +508,99 @@
     return lax.dot_general(a, b, dn, precision=HI, preferred_element_type=F32)
 
 
-def solve_kernel(alpha, g_ref, d_ref, out_ref, a, bb, li, w, u, zero):
-    zero[...] = jnp.zeros_like(zero)
-    nb = out_ref.shape[0]
+def solve_kernel(alpha, g_ref, d_ref, high_ref, low_ref, a, dg, li, u, w, zero):
+    nb = dg.shape[0]
     n = nb * 128
-    first = 0
     x = lax.axis_index("mem")
     r = lax.broadcasted_iota(jnp.int32, (128, 128), 0)
     c = lax.broadcasted_iota(jnp.int32, (128, 128), 1)
+    zero[...] = jnp.zeros_like(zero)
+    first = 0
     for i in range(nb):
         for j in range(i, nb):
             blk = g_ref[pl.ds(first, 16)].reshape(128, 128)
             first += 16
-            a[i, j] = blk + jnp.where(r == c, alpha, 0.0) if i == j else blk
+            if i == j:
+                dg[i] = blk + jnp.where(r == c, alpha, 0.0)
+            else:
+                a[i, :, pl.ds(128 * j, 128)] = blk
     unit = jnp.where(r == c, alpha * math.sqrt(n - 1.0), 0.0)
     for i in range(nb):
-        bb[i] = d_ref[pl.ds(16 * i, 16)].reshape(128, 128) + jnp.where(x == i, unit, 0.0)
+        a[i, :, pl.ds(n, 128)] = d_ref[pl.ds(16 * i, 16)].reshape(128, 128) + jnp.where(x == i, unit, 0.0)
 
     def step(b, _):
-        factor_block(a.at[b, b], li.at[b], u, zero[...])
+        factor_block(dg.at[b], li.at[b], u, zero[...])
         for s in range(nb):
 
             @pl.when(b == s)
             def _():
-                cols = [a[s, j] for j in range(s + 1, nb)] + [bb[s]]
-                us = [mm(li[s], v) for v in cols]
-                ws = [mm(u[...], v) for v in cols]
-                for t, j in enumerate(range(s + 1, nb)):
-                    w[s, j] = ws[t]
-                w[s, nb] = ws[-1]
-                for t, i in enumerate(range(s + 1, nb)):
-                    for q, j in enumerate(range(s + 1, nb)):
-                        if j >= i:
-                            a[i, j] = a[i, j] - mm(us[t], ws[q], True)
-                    bb[i] = bb[i] - mm(us[t], ws[-1], True)
+                cols = a[s, :, pl.ds(128 * (s + 1), 128 * (nb - s))]
+                us = mm(li[s], cols)
+                ws = mm(u[...], cols)
+                w[s, :, pl.ds(128 * (s + 1), 128 * (nb - s))] = ws
+                for i in range(s + 1, nb):
+                    at = 128 * (i - s - 1)
+                    change = mm(us[:, at : at + 128], ws[:, at:], True)
+                    dg[i] = dg[i] - change[:, :128]
+                    rest = pl.ds(128 * (i + 1), 128 * (nb - i))
+                    a[i, :, rest] = a[i, :, rest] - change[:, 128:]
 
         return 0
 
     lax.fori_loop(0, nb, step, 0)
     xs = [None] * nb
     for s in reversed(range(nb)):
-        acc = w[s, nb]
-        for j in range(s + 1, nb):
-            acc = acc - mm(w[s, j], xs[j])
+        acc = w[s, :, pl.ds(n, 128)]
+        if s < nb - 1:
+            acc = acc - mm(w[s, :, pl.ds(128 * (s + 1), 128 * (nb - 1 - s))], jnp.concatenate(xs[s + 1 :], axis=0))
         xs[s] = mm(li[s], acc, True)
     tot = sum(jnp.sum(v, axis=0, keepdims=True) for v in xs) * (1.0 / n)
     for s in range(nb):
-        out_ref[lax.rem(x + nb - s, nb)] = (xs[s] - tot) * (1.0 / math.sqrt(n - 1.0)) + 1.0 / n
+        at = pl.ds(pl.multiple_of(lax.rem(x + nb - s, nb) * 128, 128), 128)
+        high_ref[:, at], low_ref[:, at] = halves(((xs[s] - tot) * (1.0 / math.sqrt(n - 1.0)) + 1.0 / n).T)
 
 
 def solve(g, d, alpha):
     nb = d.shape[0] // 16
     block = (128, 128)
+    wide = pltpu.VMEM((nb, 128, 128 * (nb + 1)), F32)
     return pl.pallas_call(
         functools.partial(solve_kernel, alpha),
-        out_shape=jax.ShapeDtypeStruct((nb, *block), F32),
+        out_shape=(jax.ShapeDtypeStruct((128, 128 * nb), BF),) * 2,
         in_specs=[VM, VM],
-        out_specs=VM,
+        out_specs=(VM, VM),
         scratch_shapes=[
-            pltpu.VMEM((nb, nb, *block), F32),
+            wide,
             pltpu.VMEM((nb, *block), F32),
             pltpu.VMEM((nb, *block), F32),
-            pltpu.VMEM((nb, nb + 1, *block), F32),
             pltpu.VMEM(block, F32),
+            wide,
             pltpu.VMEM((8, 128), F32),
         ],
-        cost_estimate=pl.CostEstimate(flops=20_000_000_000, bytes_accessed=60_000_000, transcendentals=0),
         name="factor_and_solve",
     )(g, d)
 
 
-def update_kernel(u_ref, e_ref, l_ref, r_ref, o_ref, out_ref):
-    total = None
-    for d, ref in ((0, e_ref), (1, l_ref), (2, o_ref), (3, r_ref)):
-        uh, ul = halves(u_ref[d])
-        eh, el = halves(ref[...].reshape(e_ref.shape))
-        for a, b in ((uh, eh), (uh, el), (ul, eh)):
-            part = bdot(a, b, ((0,), (0,)))
-            total = part if total is None else total + part
-    out_ref[...] = total
-
-
-def update(u, e, left, right, opp):
+def update_kernel(uh_ref, ul_ref, e_ref, l_ref, o_ref, r_ref, out_ref):
+    shape = e_ref.shape
+    e = jnp.concatenate([e_ref[...]] + [ref[...].reshape(shape) for ref in (l_ref, o_ref, r_ref)], axis=0)
+    eh, el = halves(e)
+    out_ref[...] = bdot(uh_ref[...], eh) + bdot(uh_ref[...], el) + bdot(ul_ref[...], eh)
+
+
+def update(uh, ul, e, left, opp, right):
     rows, width = e.shape
     t = 512
     pair = pl.BlockSpec((2, rows // 2, t), lambda i: (0, 0, i))
+    fixed = pl.BlockSpec(uh.shape, lambda i: (0, 0))
     return pl.pallas_call(
         update_kernel,
         grid=(width // t,),
         out_shape=jax.ShapeDtypeStruct(e.shape, F32),
-        in_specs=[
-            pl.BlockSpec(u.shape, lambda i: (0, 0, 0)),
-            pl.BlockSpec((rows, t), lambda i: (0, i)),
-            pair,
-            pair,
-            pair,
-        ],
+        in_specs=[fixed, fixed, pl.BlockSpec((rows, t), lambda i: (0, i)), pair, pair, pair],
         out_specs=pl.BlockSpec((rows, t), lambda i: (0, i)),
         name="update",
-    )(u, e, left, right, opp)
+    )(uh, ul, e, left, opp, right)
 
 
 def shards(ensemble, observed, obs_sigma, obs_index, member_seeds):
@@ -599,9 +609,8 @@
     own = ensemble.shape[0]
     blocks = own * nx // 128
     width = obs_index.shape[0] // nx
-    seeds = jnp.broadcast_to(member_seeds.astype(F32)[None, :], (8, own))
     g, d, left, right, opp = reduce_all(
-        (ensemble, obs_index[None, :], seeds, observed[None, :], obs_sigma[None, :]),
+        (ensemble, obs_index[None, :], member_seeds[None, :], observed[None, :], obs_sigma[None, :]),
         all_fills(nx, alpha),
         all_scratch(own, ensemble.shape[1], width, nx),
         ensemble,
@@ -611,7 +620,7 @@
         ny,
         nz,
     )
-    return update(solve(g, d, alpha), ensemble, left, right, opp)
+    return update(*solve(g, d, alpha), ensemble, left, opp, right)
 
 
 def solution(mesh):

time: 108 us -> 106 us (0.981)
  the two profiles are of different devices: /device:TPU:32 before, /device:TPU:2 now
where the time goes in v4:
time: 106 us
  Pallas kernels  106 us (100%)
    pallas_call x1, Pallas kernels, reduce_all(): pl.pallas_call(functools.partial(reduce_kernel, (nx, ny, nz), fills, len(...  82.1 us
    pallas_call x1, Pallas kernels, solve(): pl.pallas_call(functools.partial(solve_kernel, alpha), out_shape=(jax.Sha...  19.3 us
    pallas_call x1, Pallas kernels, update(): pl.pallas_call(update_kernel, grid=(width // t,), out_shape=jax.ShapeDtyp...  4.89 us

profile of v4, /device:TPU:2, one launch (start us, length us, event | category | flops | bytes accessed | tf_op | source)
XLA Modules:
  0.0 106.3 jit_solution(949148020989342867)
XLA Ops:
  0.0 82.1 %reduce_all.1 = (f32[160,8,128]{2,1,0:T(8,128)}, f32[64,8,128]{2,1,0:T(8,128)}, f32[2,64,2048]{2,1,0:T(8,128)}, f32[2,64,2048]{2,1,0:T(8,128)}, f32[2,64,2048]{2,1,0:T(8,128)}) custom-call(f32[128,2048]{1,0:T(8,128)} %e_ref.1, s32[1,2048]{1,0:T(1,128)} %bitcast.4, s32[1,128]{1,0:T(1,128)} %bitcast.7, f32[1,2048]{1,0:T(1,128)} %bitcast.5, f32[1,2048]{1,0:T(1,128)} %bitcast.6, ...), custom_call_target="tpu_custom_call" | custom-call | tf_op jit(solution)/shard_map/reduce_all/pallas_call | solution.py:414
  82.1 19.3 %factor_and_solve.1 = (bf16[128,512]{1,0:T(8,128)(2,1)}, bf16[128,512]{1,0:T(8,128)(2,1)}) custom-call(f32[160,8,128]{2,1,0:T(8,128)} %get-tuple-element.12.g_ref, f32[64,8,128]{2,1,0:T(8,128)} %get-tuple-element.13.d_ref), custom_call_target="tpu_custom_call" | custom-call | tf_op jit(solution)/shard_map/factor_and_solve/pallas_call | solution.py:567
  101.4 4.9 %update.1 = f32[128,2048]{1,0:T(8,128)} custom-call(bf16[128,512]{1,0:T(8,128)(2,1)} %get-tuple-element.14.uh_ref, bf16[128,512]{1,0:T(8,128)(2,1)} %get-tuple-element.15.ul_ref, f32[128,2048]{1,0:T(8,128)} %e_ref.1, f32[2,64,2048]{2,1,0:T(8,128)} %get-tuple-element.16.l_ref, f32[2,64,2048]{2,1,0:T(8,128)} %get-tuple-element.17.o_ref, ...), custom_call_target="tpu_custom_call" | custom-call | tf_op jit(solution)/shard_map/update/pallas_call | solution.py:596

commit v5 on v4

--- a/solution.py
+++ b/solution.py
@@ -72,7 +72,7 @@
     x = lax.axis_index("mem")
     rows, cells = e_ref.shape
     width = i_ref.shape[1] // nx
-    step, lanes = 512, 256
+    step, lanes = 512, width // 2
 
     def split():
         mine_s[...] = jnp.broadcast_to(s_ref[0:1, :].astype(F32), mine_s.shape)
@@ -88,37 +88,32 @@
 
         lax.fori_loop(0, cells // step, block, 0)
 
-    def predict(d):
+    def predict(d, h):
         to = lax.rem(x + d, nx)
-
-        def some(h, _):
-            index = i_ref[:, pl.ds(pl.multiple_of(to * width + h * lanes, lanes), lanes)]
-
-            def fill(k, _):
-                at = pl.multiple_of(k * step, step)
-                cell = lax.broadcasted_iota(jnp.int32, (step, lanes), 0) + at
-                hot[pl.ds(at, step), :] = jnp.where(cell == index, 1.0, 0.0).astype(BF)
-                return 0
-
-            lax.fori_loop(0, cells // step, fill, 0)
-            got = bdot(parts[...], hot[...])
-            value = got[:rows] + got[rows : 2 * rows] + got[2 * rows :]
-            ready[d, :, pl.ds(pl.multiple_of(h * lanes, lanes), lanes)] = jnp.tanh(value) + 0.5 * value
+        index = i_ref[:, pl.ds(pl.multiple_of(to * width + h * lanes, lanes), lanes)]
+
+        def fill(k, _):
+            at = pl.multiple_of(k * step, step)
+            cell = lax.broadcasted_iota(jnp.int32, (step, lanes), 0) + at
+            hot[pl.ds(at, step), :] = jnp.where(cell == index, 1.0, 0.0).astype(BF)
             return 0
 
-        lax.fori_loop(0, width // lanes, some, 0)
-
-    def copies():
-        mine = pl.ds(pl.multiple_of(x * rows, rows), rows)
-        s, p = [], []
-        for d in order_of(nx):
-            there = {"mem": lax.rem(x + d, nx)}
-            s.append(remote(mine_s, seeds.at[x], send.at[1, d], recv.at[1, d], there))
-            p.append(remote(ready.at[d], o_ref.at[mine, :], send.at[0, d], recv.at[0, d], there))
-        return s, p
+        lax.fori_loop(0, cells // step, fill, 0)
+        got = bdot(parts[...], hot[...])
+        value = got[:rows] + got[rows : 2 * rows] + got[2 * rows :]
+        ready[d, h] = jnp.tanh(value) + 0.5 * value
+
+    mine = pl.ds(pl.multiple_of(x * rows, rows), rows)
+
+    def copy_of(d, h):
+        there = {"mem": lax.rem(x + d, nx)}
+        if h is None:
+            return remote(mine_s, seeds.at[x], send.at[2, d], recv.at[2, d], there)
+        return remote(ready.at[d, h], o_ref.at[h, mine, :], send.at[h, d], recv.at[h, d], there)
 
     def keep():
-        o_ref[pl.ds(pl.multiple_of(x * rows, rows), rows), :] = ready[0]
+        for h in range(2):
+            o_ref[h, mine, :] = ready[0, h]
         seeds[x] = mine_s[...]
 
     def noise():
@@ -137,42 +132,43 @@
 
         lax.fori_loop(0, nx, block, 0)
 
-    return split, predict, copies, keep, noise
+    return split, predict, copy_of, keep, noise
 
 
 def product_fills(p_ref, n_ref, ob_ref, sg_ref, gp, dp, sh, sl, mh, ml):
-    members, width = p_ref.shape
+    _, members, lanes = p_ref.shape
     blocks = members // 128
-
-    def prepare():
-        mean = jnp.sum(p_ref[...], axis=0, keepdims=True) * (1.0 / members)
-        part = pl.ds(pl.multiple_of(lax.axis_index("mem") * width, width), width)
+    both = ((1,), (1,))
+
+    def prepare(h):
+        mean = jnp.sum(p_ref[h], axis=0, keepdims=True) * (1.0 / members)
+        part = pl.ds(pl.multiple_of(lax.axis_index("mem") * 2 * lanes + h * lanes, lanes), lanes)
         inv = 1.0 / sg_ref[:, part]
         scale = inv * (1.0 / math.sqrt(members - 1.0))
         shift = (ob_ref[:, part] - mean) * inv
+        cols = pl.ds(h * lanes, lanes)
 
         def block(b, _):
             rows = pl.ds(pl.multiple_of(b * 64, 64), 64)
-            sh[rows, :], sl[rows, :] = halves((p_ref[rows, :] - mean) * scale)
-            mh[rows, :], ml[rows, :] = halves(n_ref[rows, :] + shift)
+            sh[rows, :], sl[rows, :] = halves((p_ref[h, rows, :] - mean) * scale)
+            mh[rows, :], ml[rows, :] = halves(n_ref[rows, cols] + shift)
             return 0
 
         lax.fori_loop(0, members // 64, block, 0)
 
-    both = ((1,), (1,))
-
-    def fill_d():
+    def fill_d(h):
         def block(b, _):
             rows = pl.ds(pl.multiple_of(b * 128, 128), 128)
             within = pl.ds(pl.multiple_of(lax.rem(b, 2) * 16, 16), 16)
             d = bdot(sh[rows, :], mh[...], both) + bdot(sh[rows, :], ml[...], both) + bdot(sl[rows, :], mh[...], both)
             for c in range(blocks):
-                dp[b // 2, c, within] = d[:, 128 * c : 128 * c + 128].reshape(16, 8, 128)
+                tiles = d[:, 128 * c : 128 * c + 128].reshape(16, 8, 128)
+                dp[b // 2, c, within] = dp[b // 2, c, within] + tiles if h else tiles
             return 0
 
         lax.fori_loop(0, blocks, block, 0)
 
-    def fill_g():
+    def fill_g(h):
         at = 0
         for b in range(blocks):
             rows, rest = pl.ds(128 * b, 128), pl.ds(128 * b, members - 128 * b)
@@ -183,7 +179,8 @@
                 + bdot(sl[rows, :], sl[rest, :], both)
             )
             for c in range(blocks - b):
-                gp[pl.ds(at, 16)] = g[:, 128 * c : 128 * c + 128].reshape(16, 8, 128)
+                tiles = g[:, 128 * c : 128 * c + 128].reshape(16, 8, 128)
+                gp[pl.ds(at, 16)] = gp[pl.ds(at, 16)] + tiles if h else tiles
                 at += 16
 
     return prepare, fill_d, fill_g
@@ -200,17 +197,18 @@
 def all_scratch(rows, cells, width, nx):
     dma = pltpu.SemaphoreType.DMA
     whole = (rows * nx, width)
+    lanes = width // 2
     return [
-        pltpu.VMEM(whole, F32),
+        pltpu.VMEM((2, rows * nx, lanes), F32),
         pltpu.VMEM(whole, F32),
         pltpu.VMEM((3 * rows, cells), BF),
-        pltpu.VMEM((cells, 256), BF),
-        pltpu.VMEM((nx, rows, width), F32),
+        pltpu.VMEM((cells, lanes), BF),
+        pltpu.VMEM((nx, 2, rows, lanes), F32),
         pltpu.VMEM((8, rows), F32),
         pltpu.VMEM((nx, 8, rows), F32),
-        dma((2, nx)),
-        dma((2, nx)),
-    ] + [pltpu.VMEM(whole, BF)] * 4
+        dma((3, nx)),
+        dma((3, nx)),
+    ] + [pltpu.VMEM((rows * nx, lanes), BF)] * 4
 
 
 def reduce_kernel(n, fills, n_in, *refs):
@@ -270,34 +268,43 @@
         other = e_ref.at[pl.ds((1 - h) * half, half), :]
         eo[1, h] = start(remote(other, right.at[1 - h], es.at[1, h], er.at[1, h], {"mem": xat(nx - 1)}))
 
-    split, predict, copies, keep, noise = stages
+    split, predict, copy_of, keep, noise = stages
     split()
-    for d in ox[:-1]:
-        predict(d)
-    of_seeds, of_pred = copies()
-    pl.semaphore_wait(barrier, len(peers))
-    for w in of_seeds + of_pred:
-        start(w)
+    of_seeds, of_pred = [], ([], [])
+    for h in range(2):
+        for d in ox[:-1]:
+            predict(d, h)
+            if not of_pred[0]:
+                pl.semaphore_wait(barrier, len(peers))
+                of_seeds = [start(copy_of(k, None)) for k in ox[:-1]]
+            of_pred[h].append(start(copy_of(d, h)))
     ensemble(0)
     spread()
-    predict(0)
+    predict(0, 0)
+    spread()
+    predict(0, 1)
     spread()
     keep()
     for w in of_seeds:
         w.wait_recv()
-    spread()
     noise()
     spread()
-    for w in of_pred:
+    for w in of_pred[0]:
         w.wait_recv()
-        spread()
-    prepare()
+    prepare(0)
+    spread()
+    fill_d(0)
+    spread()
+    fill_g(0)
+    for w in of_pred[1]:
+        w.wait_recv()
+    prepare(1)
+    fill_d(1)
     spread(nz)
-    fill_d()
     c0d, c0g = {}, {}
     for d in ox:
         c0d[d] = start(remote(dp.at[oc, xat(d)], rd0.at[xat(d)], cs.at[0, d], cr.at[0, d], core))
-    fill_g()
+    fill_g(1)
     for d in oy:
         c0g[d] = start(remote(gp.at[g_of(oc, yat(d))], rg0.at[yat(d)], cs.at[1, d], cr.at[1, d], core))
     d1, g1 = {}, {}
@@ -350,6 +357,12 @@
     z1 = [
         start(remote(zs.at[pl.ds(zat(d) * q, q)], rz.at[d], zss.at[0, d], zsr.at[0, d], {"cells_0": zat(d)})) for d in oz
     ]
+    eo[0, 0].wait_recv()
+    eo[1, 0].wait_recv()
+    far = [
+        start(remote(left.at[0], opp.at[0], es.at[2, 0], er.at[2, 0], {"mem": xat(1)})),
+        start(remote(right.at[1], opp.at[1], es.at[2, 1], er.at[2, 1], {"mem": xat(nx - 1)})),
+    ]
     for w in z1:
         w.wait_recv()
     own = pl.ds(z * q, q)
@@ -381,12 +394,6 @@
     for d in oy[:-1]:
         gy[d] = start(remote(go.at[go_of(y)], go.at[go_of(y)], ys.at[3, d], yr.at[3, d], {"cells_1": yat(d)}))
     last.append(start(remote(go.at[go_of(y)], go.at[go_of(y)], cs.at[3, 0], cr.at[3, 0], core)))
-    eo[0, 0].wait_recv()
-    eo[1, 0].wait_recv()
-    far = [
-        start(remote(left.at[0], opp.at[0], es.at[2, 0], er.at[2, 0], {"mem": xat(1)})),
-        start(remote(right.at[1], opp.at[1], es.at[2, 1], er.at[2, 1], {"mem": xat(nx - 1)})),
-    ]
     for d in sorted(oy[:-1]):
         dy[d].wait_recv()
         frm = do_of(yat(ny - d))

time: 106 us -> 111 us (1.047)
  the two profiles are of different devices: /device:TPU:2 before, /device:TPU:1 now
where the time goes in v5:
time: 111 us
  Pallas kernels  111 us (100%)
    pallas_call x1, Pallas kernels, reduce_all(): pl.pallas_call(functools.partial(reduce_kernel, (nx, ny, nz), fills, len(...  86.9 us
    pallas_call x1, Pallas kernels, solve(): pl.pallas_call(functools.partial(solve_kernel, alpha), out_shape=(jax.Sha...  19.3 us
    pallas_call x1, Pallas kernels, update(): pl.pallas_call(update_kernel, grid=(width // t,), out_shape=jax.ShapeDtyp...  4.89 us

profile of v5, /device:TPU:1, one launch (start us, length us, event | category | flops | bytes accessed | tf_op | source)
XLA Modules:
  0.0 111.1 jit_solution(4896078288159651216)
XLA Ops:
  0.0 86.9 %reduce_all.1 = (f32[160,8,128]{2,1,0:T(8,128)}, f32[64,8,128]{2,1,0:T(8,128)}, f32[2,64,2048]{2,1,0:T(8,128)}, f32[2,64,2048]{2,1,0:T(8,128)}, f32[2,64,2048]{2,1,0:T(8,128)}) custom-call(f32[128,2048]{1,0:T(8,128)} %e_ref.1, s32[1,2048]{1,0:T(1,128)} %bitcast.4, s32[1,128]{1,0:T(1,128)} %bitcast.7, f32[1,2048]{1,0:T(1,128)} %bitcast.5, f32[1,2048]{1,0:T(1,128)} %bitcast.6, ...), custom_call_target="tpu_custom_call" | custom-call | tf_op jit(solution)/shard_map/reduce_all/pallas_call | solution.py:421
  86.9 19.3 %factor_and_solve.1 = (bf16[128,512]{1,0:T(8,128)(2,1)}, bf16[128,512]{1,0:T(8,128)(2,1)}) custom-call(f32[160,8,128]{2,1,0:T(8,128)} %get-tuple-element.12.g_ref, f32[64,8,128]{2,1,0:T(8,128)} %get-tuple-element.13.d_ref), custom_call_target="tpu_custom_call" | custom-call | tf_op jit(solution)/shard_map/factor_and_solve/pallas_call | solution.py:574
  106.2 4.9 %update.1 = f32[128,2048]{1,0:T(8,128)} custom-call(bf16[128,512]{1,0:T(8,128)(2,1)} %get-tuple-element.14.uh_ref, bf16[128,512]{1,0:T(8,128)(2,1)} %get-tuple-element.15.ul_ref, f32[128,2048]{1,0:T(8,128)} %e_ref.1, f32[2,64,2048]{2,1,0:T(8,128)} %get-tuple-element.16.l_ref, f32[2,64,2048]{2,1,0:T(8,128)} %get-tuple-element.17.o_ref, ...), custom_call_target="tpu_custom_call" | custom-call | tf_op jit(solution)/shard_map/update/pallas_call | solution.py:603

commit v6 on v4

--- a/solution.py
+++ b/solution.py
@@ -108,14 +108,12 @@
 
         lax.fori_loop(0, width // lanes, some, 0)
 
-    def copies():
-        mine = pl.ds(pl.multiple_of(x * rows, rows), rows)
-        s, p = [], []
-        for d in order_of(nx):
-            there = {"mem": lax.rem(x + d, nx)}
-            s.append(remote(mine_s, seeds.at[x], send.at[1, d], recv.at[1, d], there))
-            p.append(remote(ready.at[d], o_ref.at[mine, :], send.at[0, d], recv.at[0, d], there))
-        return s, p
+    def copy_of(d, what):
+        there = {"mem": lax.rem(x + d, nx)}
+        if what:
+            return remote(mine_s, seeds.at[x], send.at[1, d], recv.at[1, d], there)
+        at = pl.ds(pl.multiple_of(x * rows, rows), rows)
+        return remote(ready.at[d], o_ref.at[at, :], send.at[0, d], recv.at[0, d], there)
 
     def keep():
         o_ref[pl.ds(pl.multiple_of(x * rows, rows), rows), :] = ready[0]
@@ -137,7 +135,7 @@
 
         lax.fori_loop(0, nx, block, 0)
 
-    return split, predict, copies, keep, noise
+    return split, predict, copy_of, keep, noise
 
 
 def product_fills(p_ref, n_ref, ob_ref, sg_ref, gp, dp, sh, sl, mh, ml):
@@ -213,11 +211,11 @@
     ] + [pltpu.VMEM(whole, BF)] * 4
 
 
-def reduce_kernel(n, fills, n_in, *refs):
+def reduce_kernel(n, fills, n_in, finish, *refs):
     nx, ny, nz = n
-    (e_ref, go, do, left, right, opp, gp, dp, rg0, rd0, sg0, sd0, rg1, rd1, sg1, sd1, rg2, rd2, zs, rz, zg,
-     cs, cr, xs, xr, ys, yr, zss, zsr, es, er, heard) = refs[n_in : n_in + 32]
-    stages, (prepare, fill_d, fill_g) = fills(*refs[:n_in], gp, dp, *refs[n_in + 32 :])
+    (e_ref, high, low, left, right, opp, go, do, gp, dp, rg0, rd0, sg0, sd0, rg1, rd1, sg1, sd1, rg2, rd2, zs, rz, zg,
+     cs, cr, xs, xr, ys, yr, zss, zsr, es, er, heard) = refs[n_in : n_in + 34]
+    stages, (prepare, fill_d, fill_g) = fills(*refs[:n_in], gp, dp, *refs[n_in + 34 : -6])
     z, y, c, x = (lax.axis_index(a) for a in AXES)
     oc = 1 - c
 
@@ -270,14 +268,15 @@
         other = e_ref.at[pl.ds((1 - h) * half, half), :]
         eo[1, h] = start(remote(other, right.at[1 - h], es.at[1, h], er.at[1, h], {"mem": xat(nx - 1)}))
 
-    split, predict, copies, keep, noise = stages
+    split, predict, copy_of, keep, noise = stages
     split()
+    of_seeds, of_pred = [], []
     for d in ox[:-1]:
         predict(d)
-    of_seeds, of_pred = copies()
-    pl.semaphore_wait(barrier, len(peers))
-    for w in of_seeds + of_pred:
-        start(w)
+        if not of_pred:
+            pl.semaphore_wait(barrier, len(peers))
+            of_seeds = [start(copy_of(k, True)) for k in ox[:-1]]
+        of_pred.append(start(copy_of(d, False)))
     ensemble(0)
     spread()
     predict(0)
@@ -395,13 +394,16 @@
         gy[d].wait_recv()
         frm = go_of(yat(ny - d))
         last.append(start(remote(go.at[frm], go.at[frm], cs.at[3, d], cr.at[3, d], core)))
-    for w in last + far + [eo[0, 1], eo[1, 1]]:
+    for w in last:
+        w.wait_recv()
+    finish(go, do, high, low, *refs[-6:])
+    for w in far + [eo[0, 1], eo[1, 1]]:
         w.wait_recv()
     for w in sent:
         w.wait_send()
 
 
-def reduce_all(inputs, fills, extra, e, tg, td, nx, ny, nz):
+def reduce_all(inputs, fills, extra, finish, result, more, e, tg, td, nx, ny, nz):
     q = -(-(tg + td) // nz)
     tile = (8, 128)
     m = max(nx, ny)
@@ -412,10 +414,10 @@
         return pltpu.VMEM((*lead, *tile), F32)
 
     return pl.pallas_call(
-        functools.partial(reduce_kernel, (nx, ny, nz), fills, len(inputs)),
+        functools.partial(reduce_kernel, (nx, ny, nz), fills, len(inputs), finish),
         out_shape=(
-            jax.ShapeDtypeStruct((2 * ny * nx * tg, *tile), F32),
-            jax.ShapeDtypeStruct((2 * ny * td, *tile), F32),
+            result,
+            result,
             jax.ShapeDtypeStruct(half, F32),
             jax.ShapeDtypeStruct(half, F32),
             jax.ShapeDtypeStruct(half, F32),
@@ -423,6 +425,8 @@
         in_specs=[VM] * len(inputs) + [ANY],
         out_specs=(VM, VM, ANY, ANY, ANY),
         scratch_shapes=[
+            tiles(2 * ny * nx * tg),
+            tiles(2 * ny * td),
             tiles(2 * ny * nx * tg),
             tiles(2, nx, ny * td),
             tiles(ny, nx * tg),
@@ -441,6 +445,7 @@
             dma((4, m)), dma((4, m)), dma((3, nx)), dma((3, nx)), dma((4, ny)), dma((4, ny)), dma((2, nz)), dma((2, nz)),
             dma((3, 2)), dma((3, 2)), pltpu.SemaphoreType.REGULAR((max(nz // 2 - 1, 1),)),
             *extra,
+            *more,
         ],
         compiler_params=pltpu.CompilerParams(collective_id=1, has_side_effects=True),
         name="reduce_all",
@@ -560,25 +565,17 @@
         high_ref[:, at], low_ref[:, at] = halves(((xs[s] - tot) * (1.0 / math.sqrt(n - 1.0)) + 1.0 / n).T)
 
 
-def solve(g, d, alpha):
-    nb = d.shape[0] // 16
+def solve_scratch(nb):
     block = (128, 128)
     wide = pltpu.VMEM((nb, 128, 128 * (nb + 1)), F32)
-    return pl.pallas_call(
-        functools.partial(solve_kernel, alpha),
-        out_shape=(jax.ShapeDtypeStruct((128, 128 * nb), BF),) * 2,
-        in_specs=[VM, VM],
-        out_specs=(VM, VM),
-        scratch_shapes=[
-            wide,
-            pltpu.VMEM((nb, *block), F32),
-            pltpu.VMEM((nb, *block), F32),
-            pltpu.VMEM(block, F32),
-            wide,
-            pltpu.VMEM((8, 128), F32),
-        ],
-        name="factor_and_solve",
-    )(g, d)
+    return [
+        wide,
+        pltpu.VMEM((nb, *block), F32),
+        pltpu.VMEM((nb, *block), F32),
+        pltpu.VMEM(block, F32),
+        wide,
+        pltpu.VMEM((8, 128), F32),
+    ]
 
 
 def update_kernel(uh_ref, ul_ref, e_ref, l_ref, o_ref, r_ref, out_ref):
@@ -609,10 +606,13 @@
     own = ensemble.shape[0]
     blocks = own * nx // 128
     width = obs_index.shape[0] // nx
-    g, d, left, right, opp = reduce_all(
+    high, low, left, right, opp = reduce_all(
         (ensemble, obs_index[None, :], member_seeds[None, :], observed[None, :], obs_sigma[None, :]),
         all_fills(nx, alpha),
         all_scratch(own, ensemble.shape[1], width, nx),
+        functools.partial(solve_kernel, alpha),
+        jax.ShapeDtypeStruct((128, 128 * blocks), BF),
+        solve_scratch(blocks),
         ensemble,
         16 * blocks * (blocks + 1) // 2 // (2 * ny * nx),
         16 * blocks // (2 * ny),
@@ -620,7 +620,7 @@
         ny,
         nz,
     )
-    return update(*solve(g, d, alpha), ensemble, left, opp, right)
+    return update(high, low, ensemble, left, opp, right)
 
 
 def solution(mesh):

time: 106 us -> 98.4 us (0.928)
  the two profiles are of different devices: /device:TPU:2 before, /device:TPU:1 now
where the time goes in v6:
time: 98.4 us; the launch traced here: 98.2 us
  Pallas kernels  98.2 us (100%)
    pallas_call x1, Pallas kernels, reduce_all(): pl.pallas_call(functools.partial(reduce_kernel, (nx, ny, nz), fills, len(...  93.3 us
    pallas_call x1, Pallas kernels, update(): pl.pallas_call(update_kernel, grid=(width // t,), out_shape=jax.ShapeDtyp...  4.91 us

profile of v6, /device:TPU:1, one launch (start us, length us, event | category | flops | bytes accessed | tf_op | source)
XLA Modules:
  0.0 98.2 jit_solution(13546802948979419682)
XLA Ops:
  0.0 93.3 %reduce_all.1 = (bf16[128,512]{1,0:T(8,128)(2,1)}, bf16[128,512]{1,0:T(8,128)(2,1)}, f32[2,64,2048]{2,1,0:T(8,128)}, f32[2,64,2048]{2,1,0:T(8,128)}, f32[2,64,2048]{2,1,0:T(8,128)}) custom-call(f32[128,2048]{1,0:T(8,128)} %e_ref.1, s32[1,2048]{1,0:T(1,128)} %bitcast.4, s32[1,128]{1,0:T(1,128)} %bitcast.7, f32[1,2048]{1,0:T(1,128)} %bitcast.5, ...), custom_call_target="tpu_custom_call" | custom-call | tf_op jit(solution)/shard_map/reduce_all/pallas_call | solution.py:416
  93.3 4.9 %update.1 = f32[128,2048]{1,0:T(8,128)} custom-call(bf16[128,512]{1,0:T(8,128)(2,1)} %get-tuple-element.10.uh_ref, bf16[128,512]{1,0:T(8,128)(2,1)} %get-tuple-element.11.ul_ref, f32[128,2048]{1,0:T(8,128)} %e_ref.1, f32[2,64,2048]{2,1,0:T(8,128)} %get-tuple-element.12.l_ref, f32[2,64,2048]{2,1,0:T(8,128)} %get-tuple-element.13.o_ref, ...), custom_call_target="tpu_custom_call" | custom-call | tf_op jit(solution)/shard_map/update/pallas_call | solution.py:593

commit v7 on v6

--- a/solution.py
+++ b/solution.py
@@ -213,9 +213,10 @@
 
 def reduce_kernel(n, fills, n_in, finish, *refs):
     nx, ny, nz = n
-    (e_ref, high, low, left, right, opp, go, do, gp, dp, rg0, rd0, sg0, sd0, rg1, rd1, sg1, sd1, rg2, rd2, zs, rz, zg,
-     cs, cr, xs, xr, ys, yr, zss, zsr, es, er, heard) = refs[n_in : n_in + 34]
-    stages, (prepare, fill_d, fill_g) = fills(*refs[:n_in], gp, dp, *refs[n_in + 34 : -6])
+    (e_ref, out_ref, high, low, eall, eh, el, go, do, gp, dp, rg0, rd0, sg0, sd0, rg1, rd1, sg1, sd1, rg2, rd2, zs, rz, zg,
+     cs, cr, xs, xr, ys, yr, zss, zsr, es, er, gs, gr, heard) = refs[n_in : n_in + 37]
+    stages, (prepare, fill_d, fill_g) = fills(*refs[:n_in], gp, dp, *refs[n_in + 37 : -6])
+    left, opp, right = eall.at[1], eall.at[2], eall.at[3]
     z, y, c, x = (lax.axis_index(a) for a in AXES)
     oc = 1 - c
 
@@ -349,6 +350,24 @@
     z1 = [
         start(remote(zs.at[pl.ds(zat(d) * q, q)], rz.at[d], zss.at[0, d], zsr.at[0, d], {"cells_0": zat(d)})) for d in oz
     ]
+
+    def parted(d, h):
+        rows = pl.ds((2 * d + h) * half, half)
+
+        def block(j, _):
+            cols = pl.ds(pl.multiple_of(j * 512, 512), 512)
+            source = eall[d, h, :, cols] if d else refs[0][pl.ds(h * half, half), cols]
+            eh[rows, cols], el[rows, cols] = halves(source)
+            return 0
+
+        lax.fori_loop(0, out_ref.shape[1] // 512, block, 0)
+
+    parted(0, 0)
+    parted(0, 1)
+    eo[0, 0].wait_recv()
+    eo[1, 0].wait_recv()
+    parted(1, 0)
+    parted(3, 1)
     for w in z1:
         w.wait_recv()
     own = pl.ds(z * q, q)
@@ -357,6 +376,10 @@
         total = total + rz[k]
     zg[own] = total
     z2 = [start(remote(zg.at[own], zg.at[own], zss.at[1, d], zsr.at[1, d], {"cells_0": zat(d)})) for d in oz]
+    eo[0, 1].wait_recv()
+    eo[1, 1].wait_recv()
+    parted(1, 1)
+    parted(3, 0)
     for w in z2:
         w.wait_recv()
 
@@ -369,19 +392,15 @@
     mine = pl.ds(((c * ny + y) * nx + x) * tg, tg)
     go[mine] = zg[pl.ds(td, tg)]
     do[do_of(y)] = zg[pl.ds(0, td)]
-    dy, gx, gy = {}, {}, {}
-    for d in ox[:-1]:
-        gx[d] = start(remote(zg.at[pl.ds(td, tg)], go.at[mine], xs.at[2, d], xr.at[2, d], {"mem": xat(d)}))
+    dy, gxy = {}, {}
+    for b in oy:
+        for a in ox:
+            if a or b:
+                there = {"mem": xat(a), "cells_1": yat(b)}
+                gxy[a, b] = start(remote(zg.at[pl.ds(td, tg)], go.at[mine], gs.at[b, a], gr.at[b, a], there))
     for d in oy[:-1]:
         dy[d] = start(remote(zg.at[pl.ds(0, td)], do.at[do_of(y)], ys.at[2, d], yr.at[2, d], {"cells_1": yat(d)}))
     last = [start(remote(zg.at[pl.ds(0, td)], do.at[do_of(y)], cs.at[2, 0], cr.at[2, 0], core))]
-    for d in ox[:-1]:
-        gx[d].wait_recv()
-    for d in oy[:-1]:
-        gy[d] = start(remote(go.at[go_of(y)], go.at[go_of(y)], ys.at[3, d], yr.at[3, d], {"cells_1": yat(d)}))
-    last.append(start(remote(go.at[go_of(y)], go.at[go_of(y)], cs.at[3, 0], cr.at[3, 0], core)))
-    eo[0, 0].wait_recv()
-    eo[1, 0].wait_recv()
     far = [
         start(remote(left.at[0], opp.at[0], es.at[2, 0], er.at[2, 0], {"mem": xat(1)})),
         start(remote(right.at[1], opp.at[1], es.at[2, 1], er.at[2, 1], {"mem": xat(nx - 1)})),
@@ -390,15 +409,29 @@
         dy[d].wait_recv()
         frm = do_of(yat(ny - d))
         last.append(start(remote(do.at[frm], do.at[frm], cs.at[2, d], cr.at[2, d], core)))
-    for d in reversed(oy[:-1]):
-        gy[d].wait_recv()
-        frm = go_of(yat(ny - d))
-        last.append(start(remote(go.at[frm], go.at[frm], cs.at[3, d], cr.at[3, d], core)))
+    for b in reversed(oy):
+        for a in ox:
+            if a or b:
+                gxy[a, b].wait_recv()
+        frm = go_of(yat(ny - b) if b else y)
+        last.append(start(remote(go.at[frm], go.at[frm], cs.at[3, b], cr.at[3, b], core)))
     for w in last:
         w.wait_recv()
     finish(go, do, high, low, *refs[-6:])
-    for w in far + [eo[0, 1], eo[1, 1]]:
+    for w in far:
         w.wait_recv()
+    parted(2, 0)
+    parted(2, 1)
+    wide = 512
+
+    def change(j, _):
+        cols = pl.ds(pl.multiple_of(j * wide, wide), wide)
+        out_ref[:, cols] = (
+            bdot(high[...], eh[:, cols]) + bdot(high[...], el[:, cols]) + bdot(low[...], eh[:, cols])
+        )
+        return 0
+
+    lax.fori_loop(0, out_ref.shape[1] // wide, change, 0)
     for w in sent:
         w.wait_send()
 
@@ -415,16 +448,15 @@
 
     return pl.pallas_call(
         functools.partial(reduce_kernel, (nx, ny, nz), fills, len(inputs), finish),
-        out_shape=(
+        out_shape=jax.ShapeDtypeStruct(e.shape, F32),
+        in_specs=[VM] * len(inputs) + [ANY],
+        out_specs=VM,
+        scratch_shapes=[
             result,
             result,
-            jax.ShapeDtypeStruct(half, F32),
-            jax.ShapeDtypeStruct(half, F32),
-            jax.ShapeDtypeStruct(half, F32),
-        ),
-        in_specs=[VM] * len(inputs) + [ANY],
-        out_specs=(VM, VM, ANY, ANY, ANY),
-        scratch_shapes=[
+            pltpu.VMEM((nx, *half), F32),
+            pltpu.VMEM((nx * e.shape[0], e.shape[1]), BF),
+            pltpu.VMEM((nx * e.shape[0], e.shape[1]), BF),
             tiles(2 * ny * nx * tg),
             tiles(2 * ny * td),
             tiles(2 * ny * nx * tg),
@@ -443,7 +475,7 @@
             tiles(nz, q),
             tiles(nz * q),
             dma((4, m)), dma((4, m)), dma((3, nx)), dma((3, nx)), dma((4, ny)), dma((4, ny)), dma((2, nz)), dma((2, nz)),
-            dma((3, 2)), dma((3, 2)), pltpu.SemaphoreType.REGULAR((max(nz // 2 - 1, 1),)),
+            dma((3, 2)), dma((3, 2)), dma((ny, nx)), dma((ny, nx)), pltpu.SemaphoreType.REGULAR((max(nz // 2 - 1, 1),)),
             *extra,
             *more,
         ],
@@ -578,40 +610,18 @@
     ]
 
 
-def update_kernel(uh_ref, ul_ref, e_ref, l_ref, o_ref, r_ref, out_ref):
-    shape = e_ref.shape
-    e = jnp.concatenate([e_ref[...]] + [ref[...].reshape(shape) for ref in (l_ref, o_ref, r_ref)], axis=0)
-    eh, el = halves(e)
-    out_ref[...] = bdot(uh_ref[...], eh) + bdot(uh_ref[...], el) + bdot(ul_ref[...], eh)
-
-
-def update(uh, ul, e, left, opp, right):
-    rows, width = e.shape
-    t = 512
-    pair = pl.BlockSpec((2, rows // 2, t), lambda i: (0, 0, i))
-    fixed = pl.BlockSpec(uh.shape, lambda i: (0, 0))
-    return pl.pallas_call(
-        update_kernel,
-        grid=(width // t,),
-        out_shape=jax.ShapeDtypeStruct(e.shape, F32),
-        in_specs=[fixed, fixed, pl.BlockSpec((rows, t), lambda i: (0, i)), pair, pair, pair],
-        out_specs=pl.BlockSpec((rows, t), lambda i: (0, i)),
-        name="update",
-    )(uh, ul, e, left, opp, right)
-
-
 def shards(ensemble, observed, obs_sigma, obs_index, member_seeds):
     alpha = PLAN[SECTION]
     nx, ny, nz = (lax.axis_size(a) for a in ("mem", "cells_1", "cells_0"))
     own = ensemble.shape[0]
     blocks = own * nx // 128
     width = obs_index.shape[0] // nx
-    high, low, left, right, opp = reduce_all(
+    return reduce_all(
         (ensemble, obs_index[None, :], member_seeds[None, :], observed[None, :], obs_sigma[None, :]),
         all_fills(nx, alpha),
         all_scratch(own, ensemble.shape[1], width, nx),
         functools.partial(solve_kernel, alpha),
-        jax.ShapeDtypeStruct((128, 128 * blocks), BF),
+        pltpu.VMEM((128, 128 * blocks), BF),
         solve_scratch(blocks),
         ensemble,
         16 * blocks * (blocks + 1) // 2 // (2 * ny * nx),
@@ -620,7 +630,6 @@
         ny,
         nz,
     )
-    return update(high, low, ensemble, left, opp, right)
 
 
 def solution(mesh):

time: 98.4 us -> 96.4 us (0.980)
  Pallas kernels: 98.2 us -> 94 us
  local copies, waits for them, and re-layouts: 0 us -> 2.3 us
    pallas_call x1 -> x0, Pallas kernels: 4.91 us -> none  [update(): pl.pallas_call(update_kernel, grid=(width // t,), out_shape=jax.ShapeDtyp...]
    unnamed x0 -> x1, local copies, waits for them, and re-layouts: none -> 2.3 us
where the time goes in v7:
time: 96.4 us; the launch traced here: 96.3 us
  Pallas kernels  94 us (98%)
  local copies, waits for them, and re-layouts  2.3 us (2%)
    pallas_call x1, Pallas kernels, reduce_all(): pl.pallas_call(functools.partial(reduce_kernel, (nx, ny, nz), fills, len(...  94 us
    unnamed x1, local copies, waits for them, and re-layouts  2.3 us

profile of v7, /device:TPU:1, one launch (start us, length us, event | category | flops | bytes accessed | tf_op | source)
XLA Modules:
  0.0 96.3 jit_solution(5159698512940124299)
XLA Ops:
  0.0 94.0 %reduce_all.1 = f32[128,2048]{1,0:T(8,128)} custom-call(f32[128,2048]{1,0:T(8,128)} %refs_5_.1, s32[1,2048]{1,0:T(1,128)} %bitcast.4, s32[1,128]{1,0:T(1,128)} %bitcast.7, f32[1,2048]{1,0:T(1,128)} %bitcast.5, f32[1,2048]{1,0:T(1,128)} %bitcast.6, f32[128,2048]{1,0:T(8,128)} %refs_5_.1), custom_call_target="tpu_custom_call" | custom-call | tf_op jit(solution)/shard_map/reduce_all/pallas_call | solution.py:449
  94.0 2.3 %copy.7 = f32[128,2048]{1,0:T(8,128)} copy(f32[128,2048]{1,0:T(8,128)} %reduce_all.1) | data formatting | bytes 2097152

commit v8 on v7

--- a/solution.py
+++ b/solution.py
@@ -159,8 +159,9 @@
 
     both = ((1,), (1,))
 
-    def fill_d():
-        def block(b, _):
+    def fill_d(part):
+        def block(k, _):
+            b = 2 * part + k
             rows = pl.ds(pl.multiple_of(b * 128, 128), 128)
             within = pl.ds(pl.multiple_of(lax.rem(b, 2) * 16, 16), 16)
             d = bdot(sh[rows, :], mh[...], both) + bdot(sh[rows, :], ml[...], both) + bdot(sl[rows, :], mh[...], both)
@@ -168,7 +169,7 @@
                 dp[b // 2, c, within] = d[:, 128 * c : 128 * c + 128].reshape(16, 8, 128)
             return 0
 
-        lax.fori_loop(0, blocks, block, 0)
+        lax.fori_loop(0, blocks // 2, block, 0)
 
     def fill_g():
         at = 0
@@ -293,10 +294,11 @@
         spread()
     prepare()
     spread(nz)
-    fill_d()
+    fill_d(oc)
     c0d, c0g = {}, {}
     for d in ox:
         c0d[d] = start(remote(dp.at[oc, xat(d)], rd0.at[xat(d)], cs.at[0, d], cr.at[0, d], core))
+    fill_d(c)
     fill_g()
     for d in oy:
         c0g[d] = start(remote(gp.at[g_of(oc, yat(d))], rg0.at[yat(d)], cs.at[1, d], cr.at[1, d], core))
@@ -610,13 +612,30 @@
     ]
 
 
+def place_kernel(v_ref, out_ref):
+    out_ref[...] = v_ref[...]
+
+
+def place(v):
+    rows, width = v.shape
+    block = pl.BlockSpec((rows // 2, width), lambda i: (i, 0))
+    return pl.pallas_call(
+        place_kernel,
+        grid=(2,),
+        out_shape=jax.ShapeDtypeStruct(v.shape, F32),
+        in_specs=[block],
+        out_specs=block,
+        name="place",
+    )(v)
+
+
 def shards(ensemble, observed, obs_sigma, obs_index, member_seeds):
     alpha = PLAN[SECTION]
     nx, ny, nz = (lax.axis_size(a) for a in ("mem", "cells_1", "cells_0"))
     own = ensemble.shape[0]
     blocks = own * nx // 128
     width = obs_index.shape[0] // nx
-    return reduce_all(
+    changed = reduce_all(
         (ensemble, obs_index[None, :], member_seeds[None, :], observed[None, :], obs_sigma[None, :]),
         all_fills(nx, alpha),
         all_scratch(own, ensemble.shape[1], width, nx),
@@ -630,6 +649,7 @@
         ny,
         nz,
     )
+    return place(changed)
 
 
 def solution(mesh):

time: 96.4 us -> 95.7 us (level)
  local copies, waits for them, and re-layouts: 2.3 us -> 0 us
  Pallas kernels: 94 us -> 95.5 us
    unnamed x1 -> x0, local copies, waits for them, and re-layouts: 2.3 us -> none
    pallas_call x0 -> x1, Pallas kernels: none -> 2.05 us  [place(): pl.pallas_call(place_kernel, grid=(2,), out_shape=jax.ShapeDtypeStruct(v....]
where the time goes in v8:
time: 95.7 us; the launch traced here: 95.5 us
  Pallas kernels  95.5 us (100%)
    pallas_call x1, Pallas kernels, reduce_all(): pl.pallas_call(functools.partial(reduce_kernel, (nx, ny, nz), fills, len(...  93.5 us
    pallas_call x1, Pallas kernels, place(): pl.pallas_call(place_kernel, grid=(2,), out_shape=jax.ShapeDtypeStruct(v....  2.05 us

profile of v8, /device:TPU:1, one launch (start us, length us, event | category | flops | bytes accessed | tf_op | source)
XLA Modules:
  0.0 95.5 jit_solution(3758814521530489704)
XLA Ops:
  0.0 93.5 %reduce_all.1.v_ref = f32[128,2048]{1,0:T(8,128)} custom-call(f32[128,2048]{1,0:T(8,128)} %refs_5_.1, s32[1,2048]{1,0:T(1,128)} %bitcast.4, s32[1,128]{1,0:T(1,128)} %bitcast.7, f32[1,2048]{1,0:T(1,128)} %bitcast.5, f32[1,2048]{1,0:T(1,128)} %bitcast.6, f32[128,2048]{1,0:T(8,128)} %refs_5_.1), custom_call_target="tpu_custom_call" | custom-call | tf_op jit(solution)/shard_map/reduce_all/pallas_call | solution.py:451
  93.5 2.1 %place.1 = f32[128,2048]{1,0:T(8,128)} custom-call(f32[128,2048]{1,0:T(8,128)} %reduce_all.1.v_ref), custom_call_target="tpu_custom_call" | custom-call | tf_op jit(solution)/shard_map/place/pallas_call | solution.py:622
